TPU v7x, 32 devices: a whole 2x2x4 slice. The times are simulated.
32 devices in a mesh: seq: 2 (over y), dp: 16 (over z, x, core).
Axes of the slice: x: 2, y: 2, z: 4, core: 2. Of those that a mesh axis runs over, the one named last changes fastest.
Arguments:
- tokens: bfloat16 [16, 512, 1024], P('dp', 'seq'), may hold values from -6 to 6
- starts: int32 [16, 512], P('dp', 'seq'), may hold values 0 or 1
- routes: int32 [16, 512, 8], P('dp', 'seq'), may hold values from 0 to 15, all different within a row; in each aligned block of 256 rows (0 to 255, 256 to 511, ..., all dimensions but the last counted through in order) at most 224 rows name the same one
- gain_one: bfloat16 [1024], P('dp'), may hold values from 0.5 to 1.5
- query_key_value_weight: bfloat16 [1024, 2048], P('dp'), may hold values from -0.1875 to 0.1875
- w_out: bfloat16 [1024, 1024], P('dp'), may hold values from -1.5 to 1.5
- gain_two: bfloat16 [1024], P('dp'), may hold values from 0.5 to 1.5
- w_router: bfloat16 [1024, 16], P('dp'), may hold values from -0.09375 to 0.09375
- w_gate_up: bfloat16 [1024, 16, 1024], P('dp'), may hold values from -0.1875 to 0.1875
- w_down: bfloat16 [512, 16, 1024], P('dp'), may hold values from -1 to 1
- cotangent: bfloat16 [16, 512, 1024], P('dp', 'seq'), may hold values from -6 to 6
Outputs:
- output: bfloat16 [16, 512, 1024], P('dp', 'seq')
- input_grad: bfloat16 [16, 512, 1024], P('dp', 'seq')
- grad_gain_one: float32 [1024], P('dp')
- grad_w_qkv: float32 [1024, 2048], P('dp')
- grad_w_out: float32 [1024, 1024], P('dp')
- grad_gain_two: float32 [1024], P('dp')
- grad_w_router: float32 [1024, 16], P('dp')
- grad_w_gate_up: float32 [1024, 16, 1024], P('dp')
- grad_w_down: float32 [512, 16, 1024], P('dp')
- stream_rms: float32 [16, 2], P('dp')
Inputs may be any that keep to these rules, and one draw needn't show every extreme that they name: `starts`: 1 marks a token that begins a document; a stream's first token begins one whatever its entry. `routes`: each row names 8 different experts; within the 256 rows of one device no expert is named more than 224 times, and in every draw some expert is named exactly 224 times on some device.
All inputs are finite; a program needn't handle non-finite values. No bound on the sum of `starts` on one device may be relied on, other than what follows from the above.
Results may differ from a plain program's by a relative error of at most 0.015.
Values may be sent and summed in bfloat16 or wider, within the bound.
A program may use at most 384 MiB of HBM per device.

v0:
```python
import functools

import jax
import jax.numpy as jnp
from jax import lax
from jax.experimental import pallas as pl
from jax.experimental.pallas import tpu as pltpu
from jax.sharding import PartitionSpec as P

MODEL_WIDTH = 1024
QUERY_HEADS = 16
KEY_VALUE_HEADS = 8
HEAD_SIZE = 64
F = 512
EXPERTS = 16
TOPK = 8
PLACES = 4
GROUP = 8
OWN = EXPERTS // GROUP

epsilon = 1e-06
rope_base = 10000.0
highest = lax.Precision.HIGHEST
masked_score = -1e30
f32 = jnp.float32
bf16 = jnp.bfloat16
MESH = pl.DeviceIdType.MESH

TOKEN_LINKS = ((4, 2), (2, 4))


def flip(value, bit):
    return value + bit * (1 - 2 * ((value // bit) % 2))


def flip_mask(value, mask):
    for bit in (1, 2, 4, 8):
        if mask & bit:
            value = flip(value, bit)
    return value


def subsets(bits):
    out = [0]
    for bit in bits:
        out = out + [m | bit for m in out]
    return out


def row_parts(rows):
    first = (rows // 2 + 15) // 16 * 16
    return ((0, first), (first, rows - first))


def my_place(places=PLACES):
    seq = lax.axis_index("seq")
    dp = lax.axis_index("dp")
    rank = seq * places + dp % places

    def peer(mask):
        return {
            "seq": 1 - seq if mask & places else seq,
            "dp": flip_mask(dp, mask & (places - 1)),
        }

    return rank, peer


def meet(devices):
    barrier = pltpu.get_barrier_semaphore()
    for there in devices:
        pl.semaphore_signal(barrier, inc=1, device_id=there, device_id_type=MESH)
    pl.semaphore_wait(barrier, len(devices))


def gather_kernel(count, *refs):
    ins, outs = refs[:count], refs[count : 2 * count]
    send, recv, send_core, recv_core, local = refs[2 * count :]
    rank, peer = my_place(PLACES)
    own = [
        pltpu.make_async_copy(ins[a], outs[a].at[rank], local.at[a]) for a in range(count)
    ]
    for copy in own:
        copy.start()
    meet([peer(bit) for bit in (1, 2, 4)])
    parts = [row_parts(ref.shape[0]) for ref in ins]

    def remote(a, p, mask, bit, sems, index):
        start, size = parts[a][p]
        rows = pl.ds(start, size)
        shard = flip_mask(rank, mask)
        src = ins[a].at[rows] if mask == 0 else outs[a].at[shard, rows]
        return pltpu.make_async_remote_copy(
            src_ref=src,
            dst_ref=outs[a].at[shard, rows],
            send_sem=sems[0].at[a, p, index],
            recv_sem=sems[1].at[a, p, index],
            device_id=peer(bit),
            device_id_type=MESH,
        )

    started = []
    live = {}
    for step in range(3):
        for p in range(2):
            for a in range(count):
                if parts[a][p][1] == 0:
                    continue
                order = TOKEN_LINKS[p]
                if step > 0:
                    for copy in live.pop((a, p)):
                        copy.wait_recv()
                if step < 2:
                    now = []
                    for index, mask in enumerate(subsets(order[:step])):
                        copy = remote(a, p, mask, order[step], (send, recv), 2**step - 1 + index)
                        copy.start()
                        now.append(copy)
                        started.append(copy)
                    live[(a, p)] = now
                fresh = [0] if step == 0 else [m | order[step - 1] for m in subsets(order[: step - 1])]
                base = 0 if step == 0 else 2 ** (step - 1)
                for index, mask in enumerate(fresh):
                    copy = remote(a, p, mask, 1, (send_core, recv_core), base + index)
                    copy.start()
                    live.setdefault("core", []).append(copy)
    for copy in live["core"]:
        copy.wait()
    for copy in started:
        copy.wait_send()
    for copy in own:
        copy.wait()


def group_gather(collective_id, *arrays):
    count = len(arrays)
    return pl.pallas_call(
        functools.partial(gather_kernel, count),
        out_shape=[jax.ShapeDtypeStruct((GROUP,) + a.shape, a.dtype) for a in arrays],
        in_specs=[pl.BlockSpec(memory_space=pltpu.VMEM)] * count,
        out_specs=[pl.BlockSpec(memory_space=pl.ANY)] * count,
        scratch_shapes=[
            pltpu.SemaphoreType.DMA((count, 2, 3)),
            pltpu.SemaphoreType.DMA((count, 2, 3)),
            pltpu.SemaphoreType.DMA((count, 2, 4)),
            pltpu.SemaphoreType.DMA((count, 2, 4)),
            pltpu.SemaphoreType.DMA((count,)),
        ],
        compiler_params=pltpu.CompilerParams(collective_id=collective_id, has_side_effects=True),
        cost_estimate=pl.CostEstimate(flops=1000000000, bytes_accessed=2**24, transcendentals=0),
        name="group_gather",
    )(*arrays)


def add_rows(target, source, start, size):
    def step(i, carry):
        rows = pl.ds(pl.multiple_of(start + i * 16, 16), 16)
        target[rows] = (target[rows].astype(f32) + source[rows].astype(f32)).astype(target.dtype)
        return carry

    lax.fori_loop(0, size // 16, step, 0)


def reduce_kernel(
    mixed_ref, normed_ref, gate_ref, mixed_out, normed_out, gate_out,
    total, got0, got1, got2, sems, gate_sems, local, own_gate,
):
    rank, peer = my_place(PLACES)
    chip = rank // 2
    core = rank % 2
    parts = row_parts(mixed_ref.shape[1])
    ins = (mixed_ref, normed_ref)
    outs = (mixed_out, normed_out)
    loads = []
    for t in range(2):
        for c in range(4):
            copy = pltpu.make_async_copy(ins[t].at[2 * c + core], total.at[t, c], local.at[t, c])
            copy.start()
            loads.append(copy)
    everyone = [peer(mask) for mask in range(1, GROUP)]
    meet(everyone)
    gates = []
    keep = pltpu.make_async_copy(gate_ref.at[rank], gate_out.at[rank], own_gate)
    keep.start()
    for mask, there in zip(range(1, GROUP), everyone):
        copy = pltpu.make_async_remote_copy(
            src_ref=gate_ref.at[flip_mask(rank, mask)],
            dst_ref=gate_out.at[rank],
            send_sem=gate_sems.at[0, mask],
            recv_sem=gate_sems.at[1, mask],
            device_id=there,
            device_id_type=MESH,
        )
        copy.start()
        gates.append(copy)

    started = []
    live = {}

    def send(t, p, stage, index, src, dst, bit):
        copy = pltpu.make_async_remote_copy(
            src_ref=src,
            dst_ref=dst,
            send_sem=sems.at[0, t, p, stage, index],
            recv_sem=sems.at[1, t, p, stage, index],
            device_id=peer(bit),
            device_id_type=MESH,
        )
        copy.start()
        started.append(copy)
        live.setdefault((t, p), []).append(copy)

    def chip_of(mask):
        return flip_mask(rank, mask) // 2

    for p in range(2):
        for t in range(2):
            rows = pl.ds(*parts[p])
            for c in range(4):
                send(
                    t, p, 0, c, ins[t].at[2 * c + 1 - core, rows], got0.at[t, c, rows], 1
                )
    for copy in loads:
        copy.wait()
    got = (got1, got2)
    for stage in range(3):
        for p in range(2):
            for t in range(2):
                order = TOKEN_LINKS[p]
                rows = pl.ds(*parts[p])
                for copy in live.pop((t, p)):
                    copy.wait_recv()
                if stage == 0:

                    def over_chips(c, carry, t=t, p=p):
                        add_rows(total.at[t, c], got0.at[t, c], *parts[p])
                        return carry

                    lax.fori_loop(0, 4, over_chips, 0)
                else:
                    for index, mask in enumerate(subsets(order[stage:])):
                        if stage == 2:
                            outs[t][rows] = total[t, chip, rows].astype(f32) + got2[t, 0, rows].astype(f32)
                        else:
                            add_rows(
                                total.at[t, chip_of(mask)], got[stage - 1].at[t, index], *parts[p]
                            )
                if stage < 2:
                    for index, mask in enumerate(subsets(order[stage + 1 :])):
                        send(
                            t, p, stage + 1, index,
                            total.at[t, chip_of(mask | order[stage]), rows],
                            got[stage].at[t, index, rows],
                            order[stage],
                        )
    for copy in started:
        copy.wait_send()
    for copy in gates:
        copy.wait()
    keep.wait()


def group_reduce(collective_id, mixed, normed, gate_grad):
    rows, width = mixed.shape[1:]
    return pl.pallas_call(
        reduce_kernel,
        out_shape=[
            jax.ShapeDtypeStruct((rows, width), f32),
            jax.ShapeDtypeStruct((rows, width), f32),
            jax.ShapeDtypeStruct(gate_grad.shape, gate_grad.dtype),
        ],
        in_specs=[pl.BlockSpec(memory_space=pl.ANY)] * 3,
        out_specs=[
            pl.BlockSpec(memory_space=pltpu.VMEM),
            pl.BlockSpec(memory_space=pltpu.VMEM),
            pl.BlockSpec(memory_space=pl.ANY),
        ],
        scratch_shapes=[
            pltpu.VMEM((2, 4, rows, width), bf16),
            pltpu.VMEM((2, 4, rows, width), bf16),
            pltpu.VMEM((2, 2, rows, width), bf16),
            pltpu.VMEM((2, 1, rows, width), bf16),
            pltpu.SemaphoreType.DMA((2, 2, 2, 3, 4)),
            pltpu.SemaphoreType.DMA((2, GROUP)),
            pltpu.SemaphoreType.DMA((2, 4)),
            pltpu.SemaphoreType.DMA(()),
        ],
        compiler_params=pltpu.CompilerParams(
            collective_id=collective_id, has_side_effects=True, vmem_limit_bytes=48 * 2**20
        ),
        cost_estimate=pl.CostEstimate(flops=1000000, bytes_accessed=2**24, transcendentals=0),
        name="group_reduce",
    )(mixed, normed, gate_grad)


def column_parts(half):
    first = -(-(half // 128) // 2) * 128
    return ((0, first), (first, half - first))


def shard_view(ref, halves, a, p, rank_value):
    start, size = column_parts(halves[a])[p]
    offset = pl.multiple_of((rank_value // PLACES) * halves[a] + start, 128)
    return ref.at[:, rank_value % PLACES, :, pl.ds(offset, size)]


def starts_of(sizes):
    return [sum(sizes[:i]) for i in range(len(sizes))]


def weights_gather_kernel(halves, packed, *refs):
    count = len(halves)
    outs = refs[:count]
    send, recv, local = refs[count:]
    rank, peer = my_place()
    firsts = starts_of(halves)
    seq = lax.axis_index("seq")
    own = []
    for a in range(count):
        columns = pl.ds(pl.multiple_of(seq * halves[a], 128), halves[a])
        copy = pltpu.make_async_copy(
            packed.at[:, :, pl.ds(firsts[a], halves[a])],
            outs[a].at[:, rank % PLACES, :, columns],
            local.at[a],
        )
        copy.start()
        own.append(copy)
    meet([peer(bit) for bit in (1, 2, 4)])
    started = []

    def remote(a, p, mask, bit, index):
        view = shard_view(outs[a], halves, a, p, flip_mask(rank, mask))
        start, size = column_parts(halves[a])[p]
        source = packed.at[:, :, pl.ds(firsts[a] + start, size)] if mask == 0 else view
        copy = pltpu.make_async_remote_copy(
            src_ref=source,
            dst_ref=view,
            send_sem=send.at[a, p, index],
            recv_sem=recv.at[a, p, index],
            device_id=peer(bit),
            device_id_type=MESH,
        )
        copy.start()
        started.append(copy)
        return copy

    live = {}
    last = []
    for step in range(3):
        for p in range(2):
            for a in range(count):
                if column_parts(halves[a])[p][1] == 0:
                    continue
                order = TOKEN_LINKS[p]
                if step > 0:
                    for copy in live.pop((a, p)):
                        copy.wait_recv()
                if step < 2:
                    live[(a, p)] = [
                        remote(a, p, mask, order[step], 2**step - 1 + index)
                        for index, mask in enumerate(subsets(order[:step]))
                    ]
                fresh = [0] if step == 0 else [m | order[step - 1] for m in subsets(order[: step - 1])]
                base = 0 if step == 0 else 2 ** (step - 1)
                for index, mask in enumerate(fresh):
                    last.append(remote(a, p, mask, 1, 3 + base + index))
    for copy in last:
        copy.wait_recv()
    for copy in started:
        copy.wait_send()
    for copy in own:
        copy.wait()


def weights_gather(collective_id, halves, packed):
    groups, rows, _ = packed.shape
    count = len(halves)
    whole = pl.pallas_call(
        functools.partial(weights_gather_kernel, halves),
        out_shape=[jax.ShapeDtypeStruct((groups, PLACES, rows, 2 * h), packed.dtype) for h in halves],
        in_specs=[pl.BlockSpec(memory_space=pltpu.VMEM)],
        out_specs=[pl.BlockSpec(memory_space=pl.ANY)] * count,
        scratch_shapes=[
            pltpu.SemaphoreType.DMA((count, 2, 7)),
            pltpu.SemaphoreType.DMA((count, 2, 7)),
            pltpu.SemaphoreType.DMA((count,)),
        ],
        compiler_params=pltpu.CompilerParams(collective_id=collective_id, has_side_effects=True),
        cost_estimate=pl.CostEstimate(flops=1000000, bytes_accessed=2**24, transcendentals=0),
        name="weights_gather",
    )(packed)
    return [w.reshape(-1, w.shape[3]) for w in whole]


def add_block(target, source, at, start, size):
    groups, rows = source.shape[0], source.shape[1]
    columns = pl.ds(start, size)
    pieces = rows // 16

    def step(i, carry):
        lines = pl.ds(pl.multiple_of((i % pieces) * 16, 16), 16)
        index = (i // pieces, lines, columns)
        new = target[(at,) + index].astype(f32) + source[index].astype(f32)
        target[(at,) + index] = new.astype(target.dtype)
        return carry

    lax.fori_loop(0, groups * pieces, step, 0)


def weights_reduce_kernel(count, *refs):
    ins, packed = refs[:count], refs[count]
    rest = refs[count + 1 :]
    total, got0, got1, got2 = [rest[i * count : (i + 1) * count] for i in range(4)]
    sems, local = rest[4 * count :]
    rank, peer = my_place()
    chip, core = rank // 2, rank % 2
    halves = [ref.shape[3] // 2 for ref in ins]
    firsts = starts_of(halves)
    parts = [column_parts(half) for half in halves]
    loads = []
    for a in range(count):
        for c in range(4):
            value = 2 * c + core
            offset = pl.multiple_of((value // PLACES) * halves[a], 128)
            copy = pltpu.make_async_copy(
                ins[a].at[:, value % PLACES, :, pl.ds(offset, halves[a])],
                total[a].at[c],
                local.at[a, c],
            )
            copy.start()
            loads.append(copy)
    meet([peer(bit) for bit in (1, 2, 4)])
    started = []
    live = {}

    def send(a, p, stage, index, src, dst, bit):
        copy = pltpu.make_async_remote_copy(
            src_ref=src,
            dst_ref=dst,
            send_sem=sems.at[0, a, p, stage, index],
            recv_sem=sems.at[1, a, p, stage, index],
            device_id=peer(bit),
            device_id_type=MESH,
        )
        copy.start()
        started.append(copy)
        live.setdefault((a, p), []).append(copy)

    def chip_of(mask):
        return flip_mask(rank, mask) // 2

    for p in range(2):
        for a in range(count):
            columns = pl.ds(*parts[a][p])
            if parts[a][p][1]:
                for c in range(4):
                    send(
                        a, p, 0, c,
                        shard_view(ins[a], halves, a, p, 2 * c + 1 - core),
                        got0[a].at[c, :, :, columns],
                        1,
                    )
    for copy in loads:
        copy.wait()
    got = (got1, got2)
    for stage in range(3):
        for p in range(2):
            for a in range(count):
                start, size = parts[a][p]
                if size == 0:
                    continue
                order = TOKEN_LINKS[p]
                columns = pl.ds(start, size)
                for copy in live.pop((a, p)):
                    copy.wait_recv()
                if stage == 0:

                    def over_chips(c, carry, a=a, start=start, size=size):
                        add_block(total[a], got0[a].at[c], c, start, size)
                        return carry

                    lax.fori_loop(0, 4, over_chips, 0)
                else:
                    for index, mask in enumerate(subsets(order[stage:])):
                        add_block(total[a], got[stage - 1][a].at[index], chip_of(mask), start, size)
                if stage < 2:
                    for index, mask in enumerate(subsets(order[stage + 1 :])):
                        send(
                            a, p, stage + 1, index,
                            total[a].at[chip_of(mask | order[stage]), :, :, columns],
                            got[stage][a].at[index, :, :, columns],
                            order[stage],
                        )
    for a in range(count):
        packed[:, :, pl.ds(firsts[a], halves[a])] = total[a][chip].astype(packed.dtype)
    for copy in started:
        copy.wait_send()


def weights_reduce(collective_id, groups, arrays):
    count = len(arrays)
    views = [a.reshape(groups, PLACES, -1, a.shape[1]) for a in arrays]
    rows = views[0].shape[2]
    halves = [a.shape[1] // 2 for a in arrays]

    def buffers(lead):
        return [pltpu.VMEM((lead, groups, rows, h), a.dtype) for h, a in zip(halves, arrays)]

    dma = pltpu.SemaphoreType.DMA
    return pl.pallas_call(
        functools.partial(weights_reduce_kernel, count),
        out_shape=jax.ShapeDtypeStruct((groups, rows, sum(halves)), bf16),
        in_specs=[pl.BlockSpec(memory_space=pl.ANY)] * count,
        out_specs=pl.BlockSpec(memory_space=pltpu.VMEM),
        scratch_shapes=buffers(4) + buffers(4) + buffers(2) + buffers(1)
        + [dma((2, count, 2, 3, 4)), dma((count, 4))],
        compiler_params=pltpu.CompilerParams(
            collective_id=collective_id, has_side_effects=True, vmem_limit_bytes=48 * 2**20
        ),
        cost_estimate=pl.CostEstimate(flops=1000000, bytes_accessed=2**24, transcendentals=0),
        name="weights_reduce",
    )(*views)


def pieces_kernel(pieces, packed, whole, ends, far_got, send, recv, far_send, far_recv, last, local):
    rank, peer = my_place()
    place = rank % PLACES
    groups = packed.shape[0]
    seq = lax.axis_index("seq")
    home = lax.axis_index("dp") // PLACES
    keep = pltpu.make_async_copy(pieces.at[place], whole.at[rank], local)
    keep.start()
    masks = (6, 7, 2, 4, 3, 5, 1)
    others = [(home + k) % groups for k in range(1, groups)]
    far = [{"seq": seq, "dp": g * PLACES + place} for g in others]
    meet([peer(mask) for mask in masks] + far)
    sums = []
    for k, there in enumerate(far):
        copy = pltpu.make_async_remote_copy(
            src_ref=packed.at[others[k]],
            dst_ref=far_got.at[k],
            send_sem=far_send.at[k],
            recv_sem=far_recv.at[k],
            device_id=there,
            device_id_type=MESH,
        )
        copy.start()
        sums.append(copy)
    copies = []
    for mask in masks:
        copy = pltpu.make_async_remote_copy(
            src_ref=pieces.at[flip_mask(place, mask & (PLACES - 1))],
            dst_ref=whole.at[rank],
            send_sem=send.at[mask],
            recv_sem=recv.at[mask],
            device_id=peer(mask),
            device_id_type=MESH,
        )
        copy.start()
        copies.append(copy)
    for copy in sums:
        copy.wait()
    value = packed[home].astype(f32)
    for k in range(groups - 1):
        value = value + far_got[k].astype(f32)
    ends[seq] = value.astype(ends.dtype)
    copy = pltpu.make_async_remote_copy(
        src_ref=ends.at[seq],
        dst_ref=ends.at[seq],
        send_sem=last.at[0],
        recv_sem=last.at[1],
        device_id=peer(4),
        device_id_type=MESH,
    )
    copy.start()
    copies.append(copy)
    for copy in copies:
        copy.wait()
    keep.wait()


def send_pieces(collective_id, pieces, packed):
    groups = packed.shape[0]
    others = max(groups - 1, 1)
    dma = pltpu.SemaphoreType.DMA
    vmem = pl.BlockSpec(memory_space=pltpu.VMEM)
    return pl.pallas_call(
        pieces_kernel,
        out_shape=[
            jax.ShapeDtypeStruct((GROUP,) + pieces.shape[1:], pieces.dtype),
            jax.ShapeDtypeStruct((2,) + packed.shape[1:], packed.dtype),
        ],
        in_specs=[vmem, vmem],
        out_specs=[pl.BlockSpec(memory_space=pl.ANY), vmem],
        scratch_shapes=[
            pltpu.VMEM((others,) + packed.shape[1:], packed.dtype),
            dma((GROUP,)),
            dma((GROUP,)),
            dma((others,)),
            dma((others,)),
            dma((2,)),
            dma(()),
        ],
        compiler_params=pltpu.CompilerParams(collective_id=collective_id, has_side_effects=True),
        name="send_pieces",
    )(pieces, packed)


def expert_kernel(
    first, rows_ref, grad_ref, gate_ref, weights_ref,
    mixed_ref, normed_ref, gate_grad_ref, weights_out,
    gate_up_sum, down_sum, mixed_sum, normed_sum,
):
    step = pl.program_id(0)
    expert = pl.program_id(1)
    shards, each, width = rows_ref.shape
    count = shards * each
    rows = rows_ref[...].reshape(count, width)
    grad = grad_ref[...].reshape(count, width).astype(f32)
    gate = jnp.concatenate(
        [
            jnp.broadcast_to(gate_ref[i, pl.ds(expert, 1)], (128, each)).T[:, :1]
            for i in range(shards)
        ],
        0,
    )
    gate_up_weight = weights_ref[:, expert, :first].reshape(-1, width)
    down = weights_ref[:, expert, first:].reshape(-1, width)
    gate_up = jnp.dot(rows, gate_up_weight, preferred_element_type=f32)
    gate_part, up_part = gate_up[:, :F], gate_up[:, F:]
    sigmoid = 1.0 / (1.0 + jnp.exp(-gate_part))
    silu = gate_part * sigmoid
    act = (silu * up_part).astype(bf16)
    out = jnp.dot(act, down, preferred_element_type=f32)
    inner = jnp.sum(out * grad, axis=-1, keepdims=True)
    for i in range(shards):
        line = jnp.broadcast_to(inner[i * each : (i + 1) * each], (each, 128)).T
        gate_grad_ref[i, pl.ds(expert, 1)] = line[:1]
    mixed = gate * out
    expert_grad = (gate * grad).astype(bf16)
    across = (((1,), (1,)), ((), ()))
    over_rows = (((0,), (0,)), ((), ()))
    act_grad = lax.dot_general(expert_grad, down, across, preferred_element_type=f32)
    gate_up_grad = jnp.concatenate(
        [act_grad * up_part * (sigmoid * (1.0 + gate_part * (1.0 - sigmoid))), act_grad * silu], -1
    ).astype(bf16)
    normed = lax.dot_general(gate_up_grad, gate_up_weight, across, preferred_element_type=f32)

    @pl.when(expert == 0)
    def _():
        mixed_sum[...] = mixed
        normed_sum[...] = normed

    @pl.when(expert > 0)
    def _():
        mixed_sum[...] += mixed
        normed_sum[...] += normed

    @pl.when(expert == OWN - 1)
    def _():
        mixed_ref[...] = mixed_sum[...].astype(bf16).reshape(shards, each, width)
        normed_ref[...] = normed_sum[...].astype(bf16).reshape(shards, each, width)

    @pl.when(step == 0)
    def _():
        gate_up_sum[expert] = jnp.zeros_like(gate_up_sum[0])
        down_sum[expert] = jnp.zeros_like(down_sum[0])

    down_sum[expert] += lax.dot_general(act, expert_grad, over_rows, preferred_element_type=f32)
    gate_up_sum[expert] += lax.dot_general(rows, gate_up_grad, over_rows, preferred_element_type=f32)

    @pl.when(step == pl.num_programs(0) - 1)
    def _():
        owners = weights_out.shape[0]
        weights_out[:, expert, :first] = gate_up_sum[expert].astype(bf16).reshape(owners, first, width)
        weights_out[:, expert, first:] = down_sum[expert].astype(bf16).reshape(owners, -1, width)


def expert_layer(first, rows, grad, gate, weights):
    each, width = rows.shape[1:]
    shards = 2
    owners = weights.shape[0]
    tile = pl.BlockSpec((shards, each, width), lambda i, e: (i, 0, 0))
    whole = pl.BlockSpec(weights.shape, lambda i, e: (0, 0, 0, 0), pipeline_mode=pl.Buffered(1))
    return pl.pallas_call(
        functools.partial(expert_kernel, first),
        grid=(GROUP // shards, OWN),
        out_shape=[
            jax.ShapeDtypeStruct(rows.shape, bf16),
            jax.ShapeDtypeStruct(rows.shape, bf16),
            jax.ShapeDtypeStruct((GROUP, 8, each), f32),
            jax.ShapeDtypeStruct(weights.shape, bf16),
        ],
        in_specs=[
            tile,
            tile,
            pl.BlockSpec((shards, OWN, each), lambda i, e: (i, 0, 0)),
            whole,
        ],
        out_specs=[
            tile,
            tile,
            pl.BlockSpec((shards, 8, each), lambda i, e: (i, 0, 0)),
            whole,
        ],
        scratch_shapes=[
            pltpu.VMEM((OWN, owners * first, width), f32),
            pltpu.VMEM((OWN, owners * (weights.shape[2] - first), width), f32),
            pltpu.VMEM((shards * each, width), f32),
            pltpu.VMEM((shards * each, width), f32),
        ],
        compiler_params=pltpu.CompilerParams(vmem_limit_bytes=62 * 2**20),
        cost_estimate=pl.CostEstimate(flops=45000000000, bytes_accessed=2**24, transcendentals=0),
        name="expert_layer",
    )(rows, grad, gate, weights)


def inverse_rms(rows):
    return lax.rsqrt(jnp.mean(rows * rows, axis=-1, keepdims=True) + epsilon)


def norm_back(rows, gain_row, upstream):
    inverse = inverse_rms(rows)
    gain_grad = jnp.sum(upstream * rows * inverse, axis=0)
    scaled = upstream * gain_row
    rows_grad = inverse * scaled - rows * inverse**3 * jnp.mean(scaled * rows, axis=-1, keepdims=True)
    return rows_grad, gain_grad


def rope_tables(positions):
    half = HEAD_SIZE // 2
    frequency = rope_base ** (-(jnp.arange(half, dtype=f32) * 2.0) / HEAD_SIZE)
    angles = positions.astype(f32)[:, None] * frequency[None, :]
    cosine, sine = jnp.cos(angles), jnp.sin(angles)
    return jnp.concatenate([cosine, cosine], 1), jnp.concatenate([sine, sine], 1)


def rotary_apply(rows, cosine, sine):
    half = HEAD_SIZE // 2
    turned = jnp.concatenate([-rows[..., half:], rows[..., :half]], -1)
    return rows * cosine[:, None, :] + turned * sine[:, None, :]


def unrotate(rows, cosine, sine):
    half = HEAD_SIZE // 2
    scaled = rows * sine[:, None, :]
    back = jnp.concatenate([scaled[..., half:], -scaled[..., :half]], -1)
    return rows * cosine[:, None, :] + back


def make_body(n_dp):
    expert_groups = n_dp // PLACES
    inside = [[g * PLACES + j for j in range(PLACES)] for g in range(expert_groups)]
    between = [[g * PLACES + j for g in range(expert_groups)] for j in range(PLACES)]
    half_experts = EXPERTS // 2

    def over_groups(value):
        home = lax.axis_index("dp") // PLACES

        def turned(k):
            return lax.ppermute(value, "dp", [(d, (d + k * PLACES) % n_dp) for d in range(n_dp)])

        parts = [turned(k) for k in range(expert_groups - 1, 0, -1)] + [value]
        ring = jnp.stack(parts + parts[:-1])
        start = (expert_groups - 1 - home) % expert_groups
        return lax.dynamic_slice_in_dim(ring, start, expert_groups, axis=0)

    def expert_pieces(gate_up_shard, down_shard, seq_rank):
        mine = [
            jnp.swapaxes(lax.dynamic_slice_in_dim(w, seq_rank * half_experts, half_experts, axis=1), 0, 1)
            for w in (gate_up_shard, down_shard)
        ]
        mine = jnp.concatenate(mine, 1)
        mine = mine.reshape((PLACES, OWN) + mine.shape[1:])
        return lax.all_to_all(
            mine, "dp", split_axis=0, concat_axis=0, tiled=True, axis_index_groups=inside
        )

    def body(
        tokens, starts, routes, gain_one, query_key_value_weight, w_out,
        gain_two, w_router, w_gate_up, w_down, cotangent,
    ):
        count = tokens.shape[1]
        seq_rank = lax.axis_index("seq")
        expert = (seq_rank * PLACES + lax.axis_index("dp") % PLACES) * OWN
        query_columns = QUERY_HEADS * HEAD_SIZE
        key_columns = KEY_VALUE_HEADS * HEAD_SIZE
        group = QUERY_HEADS // KEY_VALUE_HEADS
        forward_pair, back_pair = [(0, 1)], [(1, 0)]

        mine = expert_pieces(w_gate_up, w_down, seq_rank)
        tokens_before = lax.ppermute(tokens[0], "seq", forward_pair)
        starts_before = lax.ppermute(starts, "seq", forward_pair)
        spare = lambda value: jnp.pad(value, ((0, 0), (0, 128 - value.shape[1])))
        little = jnp.concatenate([spare(w_router), spare(jnp.stack([gain_one, gain_two], 1))], 1)
        shards = (query_key_value_weight, w_out, little)
        halves = [w.shape[1] // 2 for w in shards]
        packed = over_groups(
            jnp.concatenate(
                [
                    lax.dynamic_slice_in_dim(w, seq_rank * h, h, axis=1)
                    for w, h in zip(shards, halves)
                ],
                1,
            )
        )
        mine, packed, tokens_before, starts_before = lax.optimization_barrier(
            (mine, packed, tokens_before, starts_before)
        )
        weights = lax.all_gather(mine, "dp", axis=0, tiled=True, axis_index_groups=between)
        qkv_weight, out_weight, small = weights_gather(0, halves, packed)
        router_weight = small[:, :EXPERTS]
        gain_a = small[:, 128].astype(f32)
        gain_b = small[:, 129].astype(f32)

        token_rows = tokens[0].astype(f32)
        grad_output = cotangent[0].astype(f32)
        both = 2 * count
        index = jnp.arange(both, dtype=jnp.int32)
        flags = jnp.concatenate([starts_before[0], starts[0]])
        begins = (flags > 0) | (index == jnp.where(seq_rank == 0, count, 0))
        last_begin = jnp.max(
            jnp.where(begins[None, :] & (index[None, :] <= index[:, None]), index[None, :], 0), axis=1
        )
        cosine_all, sine_all = rope_tables(index - last_begin)
        cosine, sine = cosine_all[count:], sine_all[count:]

        rows_all = jnp.concatenate([tokens_before.astype(f32), token_rows], 0)
        normed_all = (rows_all * inverse_rms(rows_all) * gain_a).astype(bf16)
        normed_one = normed_all[count:]
        projected_q = jnp.dot(normed_one, qkv_weight[:, :query_columns], preferred_element_type=f32)
        projected_kv = jnp.dot(normed_all, qkv_weight[:, query_columns:], preferred_element_type=f32)
        queries = rotary_apply(
            projected_q.reshape(count, QUERY_HEADS, HEAD_SIZE), cosine, sine
        ).astype(bf16).reshape(count, KEY_VALUE_HEADS, group, HEAD_SIZE)
        keys = rotary_apply(
            projected_kv[:, :key_columns].reshape(both, KEY_VALUE_HEADS, HEAD_SIZE), cosine_all, sine_all
        ).astype(bf16)
        values = projected_kv[:, key_columns:].astype(bf16).reshape(both, KEY_VALUE_HEADS, HEAD_SIZE)

        scale = HEAD_SIZE ** (-0.5)
        allowed = (index[None, :] <= index[count:, None]) & (index[None, :] >= last_begin[count:, None])
        scores = jnp.einsum("qgrd,kgd->grqk", queries, keys, preferred_element_type=f32) * scale
        scores = jnp.where(allowed[None, None], scores, masked_score)
        top = jnp.max(scores, axis=-1, keepdims=True)
        exps = jnp.exp(scores - top)
        probs = exps / jnp.sum(exps, axis=-1, keepdims=True)
        probs_low = probs.astype(bf16)
        attended = jnp.einsum(
            "grqk,kgd->qgrd", probs_low, values, preferred_element_type=f32
        ).reshape(count, query_columns).astype(bf16)
        hidden = token_rows + jnp.dot(attended, out_weight, preferred_element_type=f32)
        normed_two = (hidden * inverse_rms(hidden) * gain_b).astype(bf16)
        logits = jnp.dot(normed_two, router_weight, preferred_element_type=f32)
        expert_ids = jnp.arange(EXPERTS, dtype=jnp.int32)
        chosen = jnp.any(routes[0][:, :, None] == expert_ids[None, None, :], axis=1)
        gates = jax.nn.softmax(jnp.where(chosen, logits, -jnp.inf), axis=-1)

        rows_in, gates_all, grad_all = group_gather(1, normed_two, gates.T, cotangent[0])
        gate = lax.dynamic_slice_in_dim(gates_all, expert, OWN, axis=1)
        mixed_part, normed_part, gate_grad_part, expert_wgrads = expert_layer(
            w_gate_up.shape[0], rows_in, grad_all, gate, weights
        )
        expert_grads = lax.psum_scatter(
            expert_wgrads, "dp", scatter_dimension=0, tiled=True, axis_index_groups=between
        )
        mixed, normed_grad, gate_grad = group_reduce(2, mixed_part, normed_part, gate_grad_part)
        gate_grad = gate_grad[:, :OWN].reshape(EXPERTS, count).T

        over_rows = (((0,), (0,)), ((), ()))
        output = (hidden + mixed).astype(bf16)[None]
        stat_sums = jnp.stack([jnp.sum(hidden * hidden), jnp.sum(mixed * mixed)])
        weighted = jnp.where(chosen, gates * gate_grad, 0.0)
        logits_grad = weighted - gates * jnp.sum(weighted, axis=-1, keepdims=True)
        router_wide = router_weight.astype(f32)
        normed_grad = normed_grad + jnp.dot(logits_grad, router_wide.T, precision=highest)
        router_wgrad = jnp.dot(normed_two.astype(f32).T, logits_grad, precision=highest)
        hidden_branch, gain_two_grad = norm_back(hidden, gain_b, normed_grad)
        hidden_grad = grad_output + hidden_branch
        branch_low = hidden_grad.astype(bf16)
        out_wgrad = lax.dot_general(attended, branch_low, over_rows, preferred_element_type=f32)
        attended_grad = lax.dot_general(
            branch_low, out_weight, (((1,), (1,)), ((), ())), preferred_element_type=f32
        ).astype(bf16).reshape(count, KEY_VALUE_HEADS, group, HEAD_SIZE)

        stat_sums = stat_sums + lax.ppermute(stat_sums, "seq", [(0, 1), (1, 0)])
        attended_grad, stat_sums = lax.optimization_barrier((attended_grad, stat_sums))
        prob_grad = jnp.einsum("qgrd,kgd->grqk", attended_grad, values, preferred_element_type=f32)
        delta = jnp.sum(probs * prob_grad, axis=-1, keepdims=True)
        score_grad = (probs * (prob_grad - delta)).astype(bf16)
        query_grad = (
            jnp.einsum("grqk,kgd->qgrd", score_grad, keys, preferred_element_type=f32) * scale
        ).reshape(count, QUERY_HEADS, HEAD_SIZE)
        key_grad = (
            jnp.einsum("grqk,qgrd->kgd", score_grad, queries, preferred_element_type=f32) * scale
        ).reshape(both, key_columns)
        value_grad = jnp.einsum(
            "grqk,qgrd->kgd", probs_low, attended_grad, preferred_element_type=f32
        ).reshape(both, key_columns)
        kv_grad = jnp.concatenate([key_grad, value_grad], 1)
        kv_back = lax.ppermute(kv_grad[:count].astype(bf16), "seq", back_pair)
        kv_grad = (kv_grad[count:] + kv_back.astype(f32)).astype(bf16).astype(f32)
        query_grad = query_grad.astype(bf16).astype(f32)
        query_back = unrotate(query_grad, cosine, sine).reshape(count, query_columns)
        key_back = unrotate(
            kv_grad[:, :key_columns].reshape(count, KEY_VALUE_HEADS, HEAD_SIZE), cosine, sine
        ).reshape(count, key_columns)
        projected_grad = jnp.concatenate([query_back, key_back, kv_grad[:, key_columns:]], 1).astype(bf16)
        qkv_wgrad = lax.dot_general(normed_one, projected_grad, over_rows, preferred_element_type=f32)
        normed_one_grad = lax.dot_general(
            projected_grad, qkv_weight, (((1,), (1,)), ((), ())), preferred_element_type=f32
        )
        rows_branch, gain_one_grad = norm_back(token_rows, gain_a, normed_one_grad)
        input_grad = (hidden_grad + rows_branch).astype(bf16)[None]

        little = jnp.concatenate(
            [spare(router_wgrad), spare(jnp.stack([gain_one_grad, gain_two_grad], 1))], 1
        )
        packed = weights_reduce(
            3, expert_groups, (qkv_wgrad.astype(bf16), out_wgrad.astype(bf16), little)
        )
        experts_all, ends = send_pieces(4, expert_grads, packed)
        qkv_shard, out_shard, little = [
            jnp.concatenate([ends[0, :, f : f + h], ends[1, :, f : f + h]], 1).astype(f32)
            for f, h in zip(starts_of(halves), halves)
        ]
        experts_all = experts_all.reshape((EXPERTS,) + experts_all.shape[2:])
        first = w_gate_up.shape[0]
        stream_rms = jnp.sqrt(stat_sums / (both * MODEL_WIDTH)).reshape(1, 2)
        return (
            output,
            input_grad,
            little[:, 128],
            qkv_shard,
            out_shard,
            little[:, 129],
            little[:, :EXPERTS],
            jnp.swapaxes(experts_all[:, :first], 0, 1).astype(f32),
            jnp.swapaxes(experts_all[:, first:], 0, 1).astype(f32),
            stream_rms,
        )

    return body


def solution(mesh):
    placed = (
        P("dp", "seq", None),
        P("dp", "seq"),
        P("dp", "seq", None),
        P("dp"),
        P("dp", None),
        P("dp", None),
        P("dp"),
        P("dp", None),
        P("dp", None, None),
        P("dp", None, None),
        P("dp", "seq", None),
    )
    return jax.shard_map(
        make_body(mesh.shape["dp"]),
        mesh=mesh,
        in_specs=placed,
        out_specs=(
            P("dp", "seq", None),
            P("dp", "seq", None),
            P("dp"),
            P("dp", None),
            P("dp", None),
            P("dp"),
            P("dp", None),
            P("dp", None, None),
            P("dp", None, None),
            P("dp", None),
        ),
        check_vma=False,
    )
```

profile of v0, /device:TPU:0, one launch (start us, length us, event | category | flops | bytes accessed | tf_op | source)
XLA Modules:
  0.0 420.9 jit_solution(17340309286261218824)
XLA Ops:
  7.2 0.8 pad_maximum_fusion.11
  8.1 0.8 copy.84
  8.9 0.9 constant_dynamic-slice_fusion.3
  9.8 0.9 constant_dynamic-slice_fusion.2
  10.7 5.1 %collective-permute-start = (bf16[64,1664]{1,0:T(8,128)(2,1)S(1)}, bf16[64,1664]{1,0:T(8,128)(2,1)S(1)}, u32[]{:S(2)}, u32[]{:S(2)}) collective-permute-start(bf16[64,1664]{1,0:T(8,128)(2,1)S(1)} %pad_maximum_fusion.8), channel_id=1, source_target_pairs={{0,12},{1,13},{2,14},{3,15},{4,0},{5,1},{6,2},{7,3},{8,4},{9,5},{1... | collective-permute-start | bytes 638984 | tf_op jit(solution)/shard_map/ppermute | solution.py:761
  15.8 1.0 collective-permute-start.2
  16.8 1.3 dynamic-slice_bitcast_fusion
  18.3 2.0 copy.83
  20.4 4.5 %all-to-all-start = ((bf16[4,2,96,1024]{3,2,1,0:T(8,128)(2,1)}), bf16[4,2,96,1024]{3,2,1,0:T(8,128)(2,1)}, u32[]{:S(2)}, u32[]{:S(2)}) async-start(bf16[4,2,96,1024]{3,2,1,0:T(8,128)(2,1)} %bitcast.186), calls=%async_computation | async-start | bytes 3145728 | tf_op jit(solution)/shard_map/all_to_all | solution.py:775
  24.9 3.5 collective-permute-start.3
  28.4 1.3 collective-permute-start.4
  29.7 4.2 collective-permute-done.1
  34.1 1.0 constant_dynamic-slice_fusion.1.packed
  35.1 5.0 %collective-permute-done.4 = s32[1,256]{1,0:T(1,128)S(1)} collective-permute-done((s32[1,256]{1,0:T(1,128)S(1)}, s32[1,256]{1,0:T(1,128)S(1)}, u32[]{:S(2)}, u32[]{:S(2)}) %collective-permute-start.4) | collective-permute-done | bytes 1056 | tf_op jit(solution)/shard_map/ppermute | solution.py:793
  40.1 4.9 %all-to-all-done = bf16[4,2,96,1024]{3,2,1,0:T(8,128)(2,1)} async-done(((bf16[4,2,96,1024]{3,2,1,0:T(8,128)(2,1)}), bf16[4,2,96,1024]{3,2,1,0:T(8,128)(2,1)}, u32[]{:S(2)}, u32[]{:S(2)}) %all-to-all-start) | async-done | bytes 1572896 | tf_op jit(solution)/shard_map/all_to_all | solution.py:775
  45.8 35.0 %weights_gather.1 = (bf16[4,4,64,2048]{3,2,1,0:T(8,128)(2,1)}, bf16[4,4,64,1024]{3,2,1,0:T(8,128)(2,1)}, bf16[4,4,64,256]{3,2,1,0:T(8,128)(2,1)}) custom-call(bf16[4,64,1664]{2,1,0:T(8,128)(2,1)} %constant_dynamic-slice_fusion.1.packed), custom_call_target="tpu_custom_call" | custom-call | flops 1000000 | bytes 16777216 | tf_op jit(solution)/shard_map/weights_gather/pallas_call | solution.py:378
  80.8 2.0 slice_convert_fusion.2
  83.5 2.1 copy-done.33
  85.6 1.3 fusion.10
  87.0 0.9 slice.235
  88.4 2.2 copy.87
  90.6 1.2 copy.115
  92.3 2.5 fusion.8
  95.1 1.0 fusion.37
  96.4 7.4 %fusion.80 = (f32[8,2,256]{2,1,0:T(2,128)S(1)}, f32[8,2,256,512]{2,3,1,0:T(8,128)}) fusion(pred[256,512]{0,1:T(8,128)(4,1)S(1)} %fusion.47, bf16[512,8,64,1]{0,2,3,1:T(8,128)(2,1)S(1)} %fusion.44, bf16[256,8,2,64]{0,3,2,1:T(8,128)(2,1)} %fusion.37), kind=kOutput, calls=%fused_computation.190 | convolution fusion | flops 276824576 | bytes 9584640 | tf_op jit(solution)/shard_map/sub | solution.py:846
  103.8 4.4 %fusion.17 = bf16[8,64,2,256]{3,1,2,0:T(8,128)(2,1)S(1)} fusion(bf16[512,8,64,1]{0,2,3,1:T(8,128)(2,1)S(1)} %bitcast.203, f32[8,2,256,512]{2,3,1,0:T(8,128)} %get-tuple-element.127, f32[8,2,256]{2,1,0:T(2,128)S(1)} %get-tuple-element.126), kind=kOutput, calls=%fused_computation.40 | convolution fusion | flops 272891904 | bytes 9453568 | tf_op jit(solution)/shard_map/grqk,kgd->qgrd/dot_general | solution.py:849
  108.2 0.8 multiply_reduce_fusion.5
  110.4 43.4 %group_gather.1 = (bf16[8,256,1024]{2,1,0:T(8,128)(2,1)}, f32[8,16,256]{2,1,0:T(8,128)}, bf16[8,256,1024]{2,1,0:T(8,128)(2,1)}) custom-call(bf16[256,1024]{1,0:T(8,128)(2,1)} %copy-done.12, f32[16,256]{1,0:T(8,128)} %fusion.77.refs_1_, bf16[256,1024]{1,0:T(8,128)(2,1)} %bitcast.202), custom_call_target="tpu_custom_call" | custom-call | flops 1000000000 | bytes 16777216 | tf_op jit(solution)/shard_map/group_gather/pallas_call | solution.py:137
  153.8 1.5 constant_dynamic-slice_fusion.gate_ref
  155.3 4.7 %all-gather.2.cloned.1.call-done.weights_ref = bf16[16,2,96,1024]{3,2,1,0:T(8,128)(2,1)} async-done(((bf16[4,2,96,1024]{3,2,1,0:T(8,128)(2,1)}), bf16[16,2,96,1024]{3,2,1,0:T(8,128)(2,1)}) %all-gather.2.cloned.1.call-update) | async-done | bytes 6291472 | tf_op jit(solution)/shard_map/all_gather | solution.py:810
  160.0 56.4 %expert_layer.1 = (bf16[8,256,1024]{2,1,0:T(8,128)(2,1)}, bf16[8,256,1024]{2,1,0:T(8,128)(2,1)}, f32[8,8,256]{2,1,0:T(8,128)}, bf16[16,2,96,1024]{3,2,1,0:T(8,128)(2,1)}) custom-call(bf16[8,256,1024]{2,1,0:T(8,128)(2,1)} %get-tuple-element.37.rows_ref, bf16[8,256,1024]{2,1,0:T(8,128)(2,1)} %get-tuple-element.38.grad_ref, ...), custom_call_target="tpu_custom_call" | custom-call | flops 44999999488 | bytes 16777216 | tf_op jit(solution)/shard_map/expert_layer/pallas_call | solution.py:685
  217.2 45.1 %group_reduce.1 = (f32[256,1024]{1,0:T(8,128)S(1)}, f32[256,1024]{1,0:T(8,128)S(1)}, f32[8,8,256]{2,1,0:T(8,128)S(1)}) custom-call(bf16[8,256,1024]{2,1,0:T(8,128)(2,1)} %get-tuple-element.41.mixed_ref, bf16[8,256,1024]{2,1,0:T(8,128)(2,1)} %get-tuple-element.42.normed_ref, f32[8,8,256]{2,1,0:T(8,128)S(1)} %copy-done.3), custom_call_target="tpu_custom_call" | custom-call | flops 1000000 | bytes 16777216 | tf_op jit(solution)/shard_map/group_reduce/pallas_call | solution.py:265
  262.5 2.6 multiply_reduce_fusion.1
  265.1 3.3 multiply_reduce_fusion.2
  268.4 1.4 pad_maximum_fusion.12
  270.3 0.8 convolution_convert_fusion.2
  271.1 1.0 copy.93
  272.4 1.8 convolution_convert_fusion.1
  274.3 1.4 fusion.102
  275.6 4.9 %fusion.1 = (f32[8,2,256]{2,1,0:T(2,128)S(1)}, f32[8,512,256,2]{2,1,3,0:T(8,128)S(1)}) fusion(f32[8,2,256,512]{2,3,1,0:T(8,128)} %get-tuple-element.127, f32[8,2,256]{2,1,0:T(2,128)S(1)} %get-tuple-element.126, bf16[512,8,64,1]{0,2,3,1:T(8,128)(2,1)S(1)} %bitcast.204, bf16[256,8,2,64]{0,3,2,1:T(8,128)(2,1)S(1)} %bitcast.205), kind=kOutput, calls=%fused_computation.3 | convolution fusion | flops 274722816 | bytes 17858560 | tf_op jit(solution)/shard_map/qgrd,kgd->grqk/dot_general | solution.py:888
  280.5 1.0 slice-done.1
  281.6 1.5 fusion.3
  283.1 1.4 fusion.16
  284.5 1.4 fusion.12
  285.9 1.7 collective-permute-start.6
  287.6 0.8 fusion.21
  289.4 12.0 %collective-permute-done.6 = bf16[256,1024]{0,1:T(8,128)(2,1)S(1)} collective-permute-done((bf16[256,1024]{0,1:T(8,128)(2,1)S(1)}, bf16[256,1024]{0,1:T(8,128)(2,1)S(1)}, u32[]{:S(2)}, u32[]{:S(2)}) %collective-permute-start.6) | collective-permute-done | bytes 524320 | tf_op jit(solution)/shard_map/ppermute | solution.py:901
  302.4 1.6 copy-done.34
  304.1 2.4 fusion.29
  306.6 1.1 select_maximum_fusion
  307.6 1.6 copy.97
  309.2 4.6 %convolution_convert_fusion = bf16[1024,2048]{1,0:T(8,128)(2,1)} fusion(bf16[512,1024]{1,0:T(8,128)(2,1)} %copy-done.19, bf16[256,512]{0,1:T(8,128)(2,1)S(1)} %copy-done.29, bf16[256,512]{0,1:T(8,128)(2,1)} %copy-done.30, bf16[256,1024]{0,1:T(8,128)(2,1)} %copy-done.26), kind=kOutput, calls=%fused_computation.14 | convolution fusion | flops 1078984704 | bytes 5767168 | tf_op jit(solution)/shard_map/dot_general | solution.py:909
  313.8 41.6 %weights_reduce.1.packed = bf16[4,64,1664]{2,1,0:T(8,128)(2,1)S(1)} custom-call(bf16[4,4,64,2048]{3,2,1,0:T(8,128)(2,1)} %bitcast.189, bf16[4,4,64,1024]{3,2,1,0:T(8,128)(2,1)S(1)} %bitcast.175, f32[4,4,64,256]{3,2,1,0:T(8,128)S(1)} %bitcast.176), custom_call_target="tpu_custom_call" | custom-call | flops 1000000 | bytes 16777216 | tf_op jit(solution)/shard_map/weights_reduce/pallas_call | solution.py:510
  355.5 0.9 copy-done.2
  356.4 1.1 fusion.45
  357.5 44.9 %send_pieces.1 = (bf16[8,2,96,1024]{3,2,1,0:T(8,128)(2,1)}, bf16[2,64,1664]{2,1,0:T(8,128)(2,1)}) custom-call(bf16[4,2,96,1024]{3,2,1,0:T(8,128)(2,1)} %reduce-scatter.2.cloned.1.call-done.pieces, bf16[4,64,1664]{2,1,0:T(8,128)(2,1)} %copy-done.2), custom_call_target="tpu_custom_call" | custom-call | tf_op jit(solution)/shard_map/send_pieces/pallas_call | solution.py:587
  402.4 1.8 slice.178
  404.2 1.4 slice.179
  405.7 0.7 slice_reduce_fusion
  406.4 3.2 convert_bitcast_fusion
  409.6 1.9 convert_bitcast_fusion.1
  411.5 0.7 copy.100
  412.2 0.7 maximum_convert_fusion.1
  412.9 0.8 maximum_convert_fusion
  (148 shorter events, 9.0 us)
Async XLA Ops:
  7.2 11.0 %copy-start = (bf16[32,16,1024]{2,1,0:T(8,128)(2,1)S(1)}, bf16[32,16,1024]{2,1,0:T(8,128)(2,1)}, u32[]{:S(2)}) copy-start(bf16[32,16,1024]{2,1,0:T(8,128)(2,1)} %param.20) | copy-start | bytes 3145732
  10.7 19.0 %collective-permute-start = (bf16[64,1664]{1,0:T(8,128)(2,1)S(1)}, bf16[64,1664]{1,0:T(8,128)(2,1)S(1)}, u32[]{:S(2)}, u32[]{:S(2)}) collective-permute-start(bf16[64,1664]{1,0:T(8,128)(2,1)S(1)} %pad_maximum_fusion.8), channel_id=1, source_target_pairs={{0,12},{1,13},{2,14},{3,15},{4,0},{5,1},{6,2},{7,3},{8,4},{9,5},{1... | collective-permute-start | bytes 638984 | tf_op jit(solution)/shard_map/ppermute | solution.py:761
  15.8 18.1 %collective-permute-start.1 = (bf16[64,1664]{1,0:T(8,128)(2,1)S(1)}, bf16[64,1664]{1,0:T(8,128)(2,1)S(1)}, u32[]{:S(2)}, u32[]{:S(2)}) collective-permute-start(bf16[64,1664]{1,0:T(8,128)(2,1)S(1)} %pad_maximum_fusion.8), channel_id=1, source_target_pairs={{0,8},{1,9},{2,10},{3,11},{4,12},{5,13},{6,14},{7,15},{8,0},{9,1},... | collective-permute-start | bytes 638984 | tf_op jit(solution)/shard_map/ppermute | solution.py:761
  15.8 18.1 %collective-permute-start.2 = (bf16[64,1664]{1,0:T(8,128)(2,1)S(1)}, bf16[64,1664]{1,0:T(8,128)(2,1)S(1)}, u32[]{:S(2)}, u32[]{:S(2)}) collective-permute-start(bf16[64,1664]{1,0:T(8,128)(2,1)S(1)} %pad_maximum_fusion.8), channel_id=1, source_target_pairs={{0,4},{1,5},{2,6},{3,7},{4,8},{5,9},{6,10},{7,11},{8,12},{9,13},{1... | collective-permute-start | bytes 638984 | tf_op jit(solution)/shard_map/ppermute | solution.py:761
  20.4 4.5 %copy-start.7 = (bf16[1,256,1024]{2,1,0:T(8,128)(2,1)S(1)}, bf16[1,256,1024]{2,1,0:T(8,128)(2,1)}, u32[]{:S(2)}) copy-start(bf16[1,256,1024]{2,1,0:T(8,128)(2,1)} %param.11) | copy-start | bytes 1572868
  20.4 8.0 %copy-start.32 = (s32[1,256]{1,0:T(1,128)S(1)}, s32[1,256]{1,0:T(1,128)}, u32[]{:S(2)}) copy-start(s32[1,256]{1,0:T(1,128)} %param.12) | copy-start | bytes 3076
  20.4 24.6 %all-to-all-start = ((bf16[4,2,96,1024]{3,2,1,0:T(8,128)(2,1)}), bf16[4,2,96,1024]{3,2,1,0:T(8,128)(2,1)}, u32[]{:S(2)}, u32[]{:S(2)}) async-start(bf16[4,2,96,1024]{3,2,1,0:T(8,128)(2,1)} %bitcast.186), calls=%async_computation | async-start | bytes 3145728 | tf_op jit(solution)/shard_map/all_to_all | solution.py:775
  24.8 135.1 %all-gather.2.cloned.1.call-start = ((), (), s32[]{:S(2)}) async-start(), calls=%async_computation.2 | async-start | bytes 7864320 | tf_op jit(solution)/shard_map/all_gather | solution.py:810
  24.9 15.2 %collective-permute-start.3 = (bf16[256,1024]{1,0:T(8,128)(2,1)S(1)}, bf16[256,1024]{1,0:T(8,128)(2,1)S(1)}, u32[]{:S(2)}, u32[]{:S(2)}) collective-permute-start(bf16[256,1024]{1,0:T(8,128)(2,1)S(1)} %bitcast.183), channel_id=1, source_target_pairs={{0,16},{1,17},{2,18},{3,19},{4,20},{5,21},{6,22},{7,23},{8,24},{9,... | collective-permute-start | bytes 1572872 | tf_op jit(solution)/shard_map/ppermute | solution.py:792
  28.4 11.7 %collective-permute-start.4 = (s32[1,256]{1,0:T(1,128)S(1)}, s32[1,256]{1,0:T(1,128)S(1)}, u32[]{:S(2)}, u32[]{:S(2)}) collective-permute-start(s32[1,256]{1,0:T(1,128)S(1)} %copy-done.32), channel_id=1, source_target_pairs={{0,16},{1,17},{2,18},{3,19},{4,20},{5,21},{6,22},{7,23},{8,24},{9,... | collective-permute-start | bytes 3080 | tf_op jit(solution)/shard_map/ppermute | solution.py:793
  34.0 11.6 %copy-start.31 = (s32[1,256,8]{1,2,0:T(8,128)S(1)}, s32[1,256,8]{1,2,0:T(8,128)}, u32[]{:S(2)}) copy-start(s32[1,256,8]{1,2,0:T(8,128)} %param.13) | copy-start | bytes 24580
  45.0 312.5 %reduce-scatter.2.cloned.1.call-start = ((), (), s32[]{:S(2)}) async-start(), calls=%async_computation.3 | async-start | bytes 7864320 | tf_op jit(solution)/shard_map/reduce_scatter | solution.py:864
  83.0 2.6 copy-start.33
  83.5 3.4 copy-start.19
  88.2 4.1 copy-start.20
  96.4 7.4 %copy-start.14 = (bf16[512,8,64,1]{0,2,3,1:T(8,128)(2,1)}, bf16[512,8,64,1]{0,2,3,1:T(8,128)(2,1)S(1)}, u32[]{:S(2)}) copy-start(bf16[512,8,64,1]{0,2,3,1:T(8,128)(2,1)S(1)} %fusion.44) | copy-start | bytes 1572868
  96.4 7.4 %copy-start.23 = (bf16[512,512]{0,1:T(8,128)(2,1)S(1)}, bf16[512,512]{0,1:T(8,128)(2,1)}, u32[]{:S(2)}) copy-start(bf16[512,512]{0,1:T(8,128)(2,1)} %copy.87) | copy-start | bytes 1572868
  103.8 4.5 %copy-start.10 = (bf16[4,4,64,1024]{3,2,1,0:T(8,128)(2,1)S(1)}, bf16[4,4,64,1024]{3,2,1,0:T(8,128)(2,1)}, u32[]{:S(2)}) copy-start(bf16[4,4,64,1024]{3,2,1,0:T(8,128)(2,1)} %get-tuple-element.36) | copy-start | bytes 6291460
  108.2 0.9 copy-start.16
  108.2 1.2 copy-start.17
  109.1 153.4 %copy-start.6 = (f32[256,1024]{1,0:T(8,128)}, f32[256,1024]{1,0:T(8,128)S(1)}, u32[]{:S(2)}) copy-start(f32[256,1024]{1,0:T(8,128)S(1)} %get-tuple-element.129) | copy-start | bytes 3145732
  109.5 0.9 copy-start.12
  216.4 0.8 copy-start.3
  262.4 2.7 copy-start.22
  265.1 5.2 %copy-start.11 = (bf16[4,4,64,1024]{3,2,1,0:T(8,128)(2,1)S(1)}, bf16[4,4,64,1024]{3,2,1,0:T(8,128)(2,1)}, u32[]{:S(2)}) copy-start(bf16[4,4,64,1024]{3,2,1,0:T(8,128)(2,1)} %get-tuple-element.36) | copy-start | bytes 6291460
  268.4 4.1 copy-start.4
  269.7 4.5 %collective-permute-start.5 = (f32[2]{0:T(128)S(1)}, f32[2]{0:T(128)S(1)}, u32[]{:S(2)}, u32[]{:S(2)}) collective-permute-start(f32[2]{0:T(128)S(1)} %pad_maximum_fusion.12), channel_id=1, source_target_pairs={{0,16},{16,0},{1,17},{17,1},{2,18},{18,2},{3,19},{19,3},{4,20},{20... | collective-permute-start | bytes 32 | tf_op jit(solution)/shard_map/ppermute | solution.py:886
  270.3 1.8 copy-start.13
  272.1 3.5 copy-start.24
  272.1 3.5 copy-start.25
  275.6 4.9 %slice-start = ((s8[8388608]{0:T(1024)(128)(4,1)}), s8[4194304]{0:T(1024)(128)(4,1)S(1)}, s32[]{:S(2)}) async-start(s8[8388608]{0:T(1024)(128)(4,1)} %bitcast.181), calls=%async_computation.4 | async-start | bytes 8388608
  275.6 5.9 %slice-start.1 = ((s8[8388608]{0:T(1024)(128)(4,1)}), s8[4194304]{0:T(1024)(128)(4,1)S(1)}, s32[]{:S(2)}) async-start(s8[8388608]{0:T(1024)(128)(4,1)} %bitcast.181), calls=%async_computation.5 | async-start | bytes 8388608
  281.6 1.5 copy-start.18
  285.9 1.8 copy-start.15
  285.9 15.5 %collective-permute-start.6 = (bf16[256,1024]{0,1:T(8,128)(2,1)S(1)}, bf16[256,1024]{0,1:T(8,128)(2,1)S(1)}, u32[]{:S(2)}, u32[]{:S(2)}) collective-permute-start(bf16[256,1024]{0,1:T(8,128)(2,1)S(1)} %fusion.33), channel_id=1, source_target_pairs={{16,0},{17,1},{18,2},{19,3},{20,4},{21,5},{22,6},{23,7},{24,8},{25... | collective-permute-start | bytes 1572872 | tf_op jit(solution)/shard_map/ppermute | solution.py:901
  288.9 13.1 %copy-start.26 = (bf16[256,1024]{0,1:T(8,128)(2,1)}, bf16[256,1024]{0,1:T(8,128)(2,1)S(1)}, u32[]{:S(2)}) copy-start(bf16[256,1024]{0,1:T(8,128)(2,1)S(1)} %fusion.39) | copy-start | bytes 1572868
  301.6 2.4 copy-start.34
  301.7 0.7 copy-start.28
  301.7 2.4 copy-start.8
  301.9 4.6 %copy-start.30 = (bf16[256,512]{0,1:T(8,128)(2,1)}, bf16[256,512]{0,1:T(8,128)(2,1)S(1)}, u32[]{:S(2)}) copy-start(bf16[256,512]{0,1:T(8,128)(2,1)S(1)} %fusion.46) | copy-start | bytes 786436
  306.5 2.7 copy-start.29
  313.8 42.5 %copy-start.5 = (f32[256,1024]{1,0:T(8,128)S(1)}, f32[256,1024]{1,0:T(8,128)}, u32[]{:S(2)}) copy-start(f32[256,1024]{1,0:T(8,128)} %copy-done.4) | copy-start | bytes 3145732
  313.8 42.5 %copy-start.9 = (bf16[1,256,1024]{2,1,0:T(8,128)(2,1)S(1)}, bf16[1,256,1024]{2,1,0:T(8,128)(2,1)}, u32[]{:S(2)}) copy-start(bf16[1,256,1024]{2,1,0:T(8,128)(2,1)} %param.11) | copy-start | bytes 1572868
  313.8 42.5 %copy-start.21 = (f32[256,1024]{1,0:T(8,128)S(1)}, f32[256,1024]{1,0:T(8,128)}, u32[]{:S(2)}) copy-start(f32[256,1024]{1,0:T(8,128)} %get-tuple-element.135) | copy-start | bytes 3145732
  355.5 0.9 copy-start.2
  404.2 1.4 copy-start.27
  406.4 7.4 %copy-start.1 = (bf16[32,16,1024]{2,1,0:T(8,128)(2,1)S(1)}, bf16[32,16,1024]{2,1,0:T(8,128)(2,1)}, u32[]{:S(2)}) copy-start(bf16[32,16,1024]{2,1,0:T(8,128)(2,1)} %param.20) | copy-start | bytes 3145732
Sparse Core Ops, SparseCore 0:
  45.1 114.8 all-gather.1
  216.5 108.9 reduce-scatter.1
where the time goes:
time: 424 us; the launch traced here: 421 us
  Pallas kernels  266 us (63%)
  matrix products  37.6 us (9%)
  waiting for transfers between devices  30.8 us (7%)
  local copies, waits for them, and re-layouts  27.7 us (7%)
  other arithmetic  24.8 us (6%)
  starting transfers between devices  18.2 us (4%)
  between operations  15.3 us (4%)
    pallas_call x1, Pallas kernels, expert_layer(): pl.pallas_call(functools.partial(expert_kernel, first), grid=(GROUP // sh...  56.4 us
    pallas_call x1, Pallas kernels, group_reduce(): pl.pallas_call(reduce_kernel, out_shape=[jax.ShapeDtypeStruct((rows, widt...  45.1 us
    pallas_call x1, Pallas kernels, send_pieces(): pl.pallas_call(pieces_kernel, out_shape=[jax.ShapeDtypeStruct((GROUP,) +...  44.9 us
    pallas_call x1, Pallas kernels, group_gather(): pl.pallas_call(functools.partial(gather_kernel, count), out_shape=[jax.Sh...  43.4 us
    pallas_call x1, Pallas kernels, weights_reduce(): pl.pallas_call(functools.partial(weights_reduce_kernel, count), out_shape...  41.6 us
    pallas_call x1, Pallas kernels, weights_gather(): pl.pallas_call(functools.partial(weights_gather_kernel, halves), out_shap...  35 us
    ppermute x1, waiting for transfers between devices, body(): kv_back = lax.ppermute(kv_grad[:count].astype(bf16), 'seq', back_pair)  12 us
    unnamed x83, local copies, waits for them, and re-layouts  10.1 us
  transfers between devices with their start and end apart: 10, of which 5 were waited for; matrix products, arithmetic and copies ran while one was open for 16% of the time, Pallas kernels for 39%

commit v1 on v0

--- a/solution.py
+++ b/solution.py
@@ -162,17 +162,17 @@
 
 
 def reduce_kernel(
-    mixed_ref, normed_ref, gate_ref, mixed_out, normed_out, gate_out,
+    normed_ref, gate_ref, normed_out, gate_out,
     total, got0, got1, got2, sems, gate_sems, local, own_gate,
 ):
     rank, peer = my_place(PLACES)
     chip = rank // 2
     core = rank % 2
-    parts = row_parts(mixed_ref.shape[1])
-    ins = (mixed_ref, normed_ref)
-    outs = (mixed_out, normed_out)
+    parts = row_parts(normed_ref.shape[1])
+    ins = (normed_ref,)
+    outs = (normed_out,)
     loads = []
-    for t in range(2):
+    for t in range(1):
         for c in range(4):
             copy = pltpu.make_async_copy(ins[t].at[2 * c + core], total.at[t, c], local.at[t, c])
             copy.start()
@@ -214,7 +214,7 @@
         return flip_mask(rank, mask) // 2
 
     for p in range(2):
-        for t in range(2):
+        for t in range(1):
             rows = pl.ds(*parts[p])
             for c in range(4):
                 send(
@@ -225,7 +225,7 @@
     got = (got1, got2)
     for stage in range(3):
         for p in range(2):
-            for t in range(2):
+            for t in range(1):
                 order = TOKEN_LINKS[p]
                 rows = pl.ds(*parts[p])
                 for copy in live.pop((t, p)):
@@ -260,29 +260,27 @@
     keep.wait()
 
 
-def group_reduce(collective_id, mixed, normed, gate_grad):
-    rows, width = mixed.shape[1:]
+def group_reduce(collective_id, normed, gate_grad):
+    rows, width = normed.shape[1:]
     return pl.pallas_call(
         reduce_kernel,
         out_shape=[
             jax.ShapeDtypeStruct((rows, width), f32),
-            jax.ShapeDtypeStruct((rows, width), f32),
             jax.ShapeDtypeStruct(gate_grad.shape, gate_grad.dtype),
         ],
-        in_specs=[pl.BlockSpec(memory_space=pl.ANY)] * 3,
+        in_specs=[pl.BlockSpec(memory_space=pl.ANY)] * 2,
         out_specs=[
             pl.BlockSpec(memory_space=pltpu.VMEM),
-            pl.BlockSpec(memory_space=pltpu.VMEM),
             pl.BlockSpec(memory_space=pl.ANY),
         ],
         scratch_shapes=[
-            pltpu.VMEM((2, 4, rows, width), bf16),
-            pltpu.VMEM((2, 4, rows, width), bf16),
-            pltpu.VMEM((2, 2, rows, width), bf16),
-            pltpu.VMEM((2, 1, rows, width), bf16),
-            pltpu.SemaphoreType.DMA((2, 2, 2, 3, 4)),
+            pltpu.VMEM((1, 4, rows, width), bf16),
+            pltpu.VMEM((1, 4, rows, width), bf16),
+            pltpu.VMEM((1, 2, rows, width), bf16),
+            pltpu.VMEM((1, 1, rows, width), bf16),
+            pltpu.SemaphoreType.DMA((2, 1, 2, 3, 4)),
             pltpu.SemaphoreType.DMA((2, GROUP)),
-            pltpu.SemaphoreType.DMA((2, 4)),
+            pltpu.SemaphoreType.DMA((1, 4)),
             pltpu.SemaphoreType.DMA(()),
         ],
         compiler_params=pltpu.CompilerParams(
@@ -290,7 +288,7 @@
         ),
         cost_estimate=pl.CostEstimate(flops=1000000, bytes_accessed=2**24, transcendentals=0),
         name="group_reduce",
-    )(mixed, normed, gate_grad)
+    )(normed, gate_grad)
 
 
 def column_parts(half):
@@ -408,24 +406,28 @@
 
 
 def weights_reduce_kernel(count, *refs):
-    ins, packed = refs[:count], refs[count]
-    rest = refs[count + 1 :]
+    ins, packed, rows_out = refs[:count], refs[count], refs[count + 1]
+    rest = refs[count + 2 :]
     total, got0, got1, got2 = [rest[i * count : (i + 1) * count] for i in range(4)]
     sems, local = rest[4 * count :]
     rank, peer = my_place()
     chip, core = rank // 2, rank % 2
-    halves = [ref.shape[3] // 2 for ref in ins]
+    halves = [ref.shape[3] // 2 for ref in ins[:-1]]
     firsts = starts_of(halves)
+    halves = halves + [ins[-1].shape[3]]
     parts = [column_parts(half) for half in halves]
+
+    def source(a, value, start, size):
+        if a == count - 1:
+            return ins[a].at[value, :, :, pl.ds(start, size)]
+        offset = pl.multiple_of((value // PLACES) * halves[a] + start, 128)
+        return ins[a].at[:, value % PLACES, :, pl.ds(offset, size)]
+
     loads = []
     for a in range(count):
         for c in range(4):
-            value = 2 * c + core
-            offset = pl.multiple_of((value // PLACES) * halves[a], 128)
             copy = pltpu.make_async_copy(
-                ins[a].at[:, value % PLACES, :, pl.ds(offset, halves[a])],
-                total[a].at[c],
-                local.at[a, c],
+                source(a, 2 * c + core, 0, halves[a]), total[a].at[c], local.at[a, c]
             )
             copy.start()
             loads.append(copy)
@@ -456,7 +458,7 @@
                 for c in range(4):
                     send(
                         a, p, 0, c,
-                        shard_view(ins[a], halves, a, p, 2 * c + 1 - core),
+                        source(a, 2 * c + 1 - core, *parts[a][p]),
                         got0[a].at[c, :, :, columns],
                         1,
                     )
@@ -491,27 +493,36 @@
                             got[stage][a].at[index, :, :, columns],
                             order[stage],
                         )
-    for a in range(count):
+    for a in range(count - 1):
         packed[:, :, pl.ds(firsts[a], halves[a])] = total[a][chip].astype(packed.dtype)
+    rows_out[...] = total[-1][chip]
     for copy in started:
         copy.wait_send()
 
 
-def weights_reduce(collective_id, groups, arrays):
-    count = len(arrays)
+def weights_reduce(collective_id, groups, arrays, token_rows):
+    count = len(arrays) + 1
     views = [a.reshape(groups, PLACES, -1, a.shape[1]) for a in arrays]
     rows = views[0].shape[2]
     halves = [a.shape[1] // 2 for a in arrays]
 
+    each, width = token_rows.shape[1:]
+    token_shape = (groups, each // groups, width)
+
     def buffers(lead):
-        return [pltpu.VMEM((lead, groups, rows, h), a.dtype) for h, a in zip(halves, arrays)]
+        return [pltpu.VMEM((lead, groups, rows, h), a.dtype) for h, a in zip(halves, arrays)] + [
+            pltpu.VMEM((lead,) + token_shape, bf16)
+        ]
 
     dma = pltpu.SemaphoreType.DMA
     return pl.pallas_call(
         functools.partial(weights_reduce_kernel, count),
-        out_shape=jax.ShapeDtypeStruct((groups, rows, sum(halves)), bf16),
+        out_shape=[
+            jax.ShapeDtypeStruct((groups, rows, sum(halves)), bf16),
+            jax.ShapeDtypeStruct(token_shape, bf16),
+        ],
         in_specs=[pl.BlockSpec(memory_space=pl.ANY)] * count,
-        out_specs=pl.BlockSpec(memory_space=pltpu.VMEM),
+        out_specs=[pl.BlockSpec(memory_space=pltpu.VMEM)] * 2,
         scratch_shapes=buffers(4) + buffers(4) + buffers(2) + buffers(1)
         + [dma((2, count, 2, 3, 4)), dma((count, 4))],
         compiler_params=pltpu.CompilerParams(
@@ -519,7 +530,7 @@
         ),
         cost_estimate=pl.CostEstimate(flops=1000000, bytes_accessed=2**24, transcendentals=0),
         name="weights_reduce",
-    )(*views)
+    )(*views, token_rows.reshape((GROUP,) + token_shape))
 
 
 def pieces_kernel(pieces, packed, whole, ends, far_got, send, recv, far_send, far_recv, last, local):
@@ -771,10 +782,7 @@
             for w in (gate_up_shard, down_shard)
         ]
         mine = jnp.concatenate(mine, 1)
-        mine = mine.reshape((PLACES, OWN) + mine.shape[1:])
-        return lax.all_to_all(
-            mine, "dp", split_axis=0, concat_axis=0, tiled=True, axis_index_groups=inside
-        )
+        return mine.reshape((PLACES, OWN) + mine.shape[1:])
 
     def body(
         tokens, starts, routes, gain_one, query_key_value_weight, w_out,
@@ -789,6 +797,12 @@
         forward_pair, back_pair = [(0, 1)], [(1, 0)]
 
         mine = expert_pieces(w_gate_up, w_down, seq_rank)
+        mine, query_key_value_weight, tokens, starts = lax.optimization_barrier(
+            (mine, query_key_value_weight, tokens, starts)
+        )
+        mine = lax.all_to_all(
+            mine, "dp", split_axis=0, concat_axis=0, tiled=True, axis_index_groups=inside
+        )
         tokens_before = lax.ppermute(tokens[0], "seq", forward_pair)
         starts_before = lax.ppermute(starts, "seq", forward_pair)
         spare = lambda value: jnp.pad(value, ((0, 0), (0, 128 - value.shape[1])))
@@ -864,12 +878,10 @@
         expert_grads = lax.psum_scatter(
             expert_wgrads, "dp", scatter_dimension=0, tiled=True, axis_index_groups=between
         )
-        mixed, normed_grad, gate_grad = group_reduce(2, mixed_part, normed_part, gate_grad_part)
+        normed_grad, gate_grad = group_reduce(2, normed_part, gate_grad_part)
         gate_grad = gate_grad[:, :OWN].reshape(EXPERTS, count).T
 
         over_rows = (((0,), (0,)), ((), ()))
-        output = (hidden + mixed).astype(bf16)[None]
-        stat_sums = jnp.stack([jnp.sum(hidden * hidden), jnp.sum(mixed * mixed)])
         weighted = jnp.where(chosen, gates * gate_grad, 0.0)
         logits_grad = weighted - gates * jnp.sum(weighted, axis=-1, keepdims=True)
         router_wide = router_weight.astype(f32)
@@ -883,8 +895,6 @@
             branch_low, out_weight, (((1,), (1,)), ((), ())), preferred_element_type=f32
         ).astype(bf16).reshape(count, KEY_VALUE_HEADS, group, HEAD_SIZE)
 
-        stat_sums = stat_sums + lax.ppermute(stat_sums, "seq", [(0, 1), (1, 0)])
-        attended_grad, stat_sums = lax.optimization_barrier((attended_grad, stat_sums))
         prob_grad = jnp.einsum("qgrd,kgd->grqk", attended_grad, values, preferred_element_type=f32)
         delta = jnp.sum(probs * prob_grad, axis=-1, keepdims=True)
         score_grad = (probs * (prob_grad - delta)).astype(bf16)
@@ -916,9 +926,13 @@
         little = jnp.concatenate(
             [spare(router_wgrad), spare(jnp.stack([gain_one_grad, gain_two_grad], 1))], 1
         )
-        packed = weights_reduce(
-            3, expert_groups, (qkv_wgrad.astype(bf16), out_wgrad.astype(bf16), little)
-        )
+        packed, mixed = weights_reduce(
+            3, expert_groups, (qkv_wgrad.astype(bf16), out_wgrad.astype(bf16), little), mixed_part
+        )
+        mixed = mixed.reshape(count, MODEL_WIDTH).astype(f32)
+        output = (hidden + mixed).astype(bf16)[None]
+        stat_sums = jnp.stack([jnp.sum(hidden * hidden), jnp.sum(mixed * mixed)])
+        stat_sums = stat_sums + lax.ppermute(stat_sums, "seq", [(0, 1), (1, 0)])
         experts_all, ends = send_pieces(4, expert_grads, packed)
         qkv_shard, out_shard, little = [
             jnp.concatenate([ends[0, :, f : f + h], ends[1, :, f : f + h]], 1).astype(f32)

time: 424 us -> 426 us (level)
  waiting for transfers between devices: 30.8 us -> 38.3 us
    pallas_call x1, Pallas kernels: 41.6 us -> 59.3 us  [weights_reduce(): pl.pallas_call(functools.partial(weights_reduce_kernel, count), out_shape...]
    pallas_call x1, Pallas kernels: 45.1 us -> 27.9 us  [group_reduce(): pl.pallas_call(reduce_kernel, out_shape=[jax.ShapeDtypeStruct((rows, widt...]
    all_to_all x1, waiting for transfers between devices: 4.85 us -> 10.9 us  [body(): lax.all_to_all(mine, 'dp', split_axis=0, concat_axis=0, tiled=True, axis_...]
    ppermute x1, waiting for transfers between devices: 5.01 us -> 0.01 us  [body(): starts_before = lax.ppermute(starts, 'seq', forward_pair)]
    unnamed x83 -> x93, local copies, waits for them, and re-layouts: 10.1 us -> 14.4 us
  transfers between devices with their start and end apart: 10 -> 10, of which waited for: 5 -> 5; matrix products, arithmetic and copies ran while one was open for 16% -> 15% of each run, Pallas kernels for 39% -> 39%
where the time goes in v1:
time: 426 us; the launch traced here: 425 us
  Pallas kernels  266 us (62%)
  waiting for transfers between devices  38.3 us (9%)
  matrix products  34.5 us (8%)
  local copies, waits for them, and re-layouts  29.4 us (7%)
  other arithmetic  25.3 us (6%)
  starting transfers between devices  16.8 us (4%)
  between operations  15 us (4%)
    pallas_call x1, Pallas kernels, weights_reduce(): pl.pallas_call(functools.partial(weights_reduce_kernel, count), out_shape...  59.3 us
    pallas_call x1, Pallas kernels, expert_layer(): pl.pallas_call(functools.partial(expert_kernel, first), grid=(GROUP // sh...  56.2 us
    pallas_call x1, Pallas kernels, send_pieces(): pl.pallas_call(pieces_kernel, out_shape=[jax.ShapeDtypeStruct((GROUP,) +...  44.8 us
    pallas_call x1, Pallas kernels, group_gather(): pl.pallas_call(functools.partial(gather_kernel, count), out_shape=[jax.Sh...  42.9 us
    pallas_call x1, Pallas kernels, weights_gather(): pl.pallas_call(functools.partial(weights_gather_kernel, halves), out_shap...  34.7 us
    pallas_call x1, Pallas kernels, group_reduce(): pl.pallas_call(reduce_kernel, out_shape=[jax.ShapeDtypeStruct((rows, widt...  27.9 us
    unnamed x93, local copies, waits for them, and re-layouts  14.4 us
    ppermute x1, waiting for transfers between devices, body(): kv_back = lax.ppermute(kv_grad[:count].astype(bf16), 'seq', back_pair)  12.8 us
  transfers between devices with their start and end apart: 10, of which 5 were waited for; matrix products, arithmetic and copies ran while one was open for 15% of the time, Pallas kernels for 39%

profile of v1, /device:TPU:0, one launch (start us, length us, event | category | flops | bytes accessed | tf_op | source)
XLA Modules:
  0.0 425.1 jit_solution(15359969714976771956)
XLA Ops:
  7.2 1.4 dynamic-slice_bitcast_fusion
  9.0 2.0 copy.83
  11.4 5.1 %collective-permute-start = (bf16[64,1664]{1,0:T(8,128)(2,1)S(1)}, bf16[64,1664]{1,0:T(8,128)(2,1)S(1)}, u32[]{:S(2)}, u32[]{:S(2)}) collective-permute-start(bf16[64,1664]{1,0:T(8,128)(2,1)S(1)} %pad_maximum_fusion.8), channel_id=1, source_target_pairs={{0,12},{1,13},{2,14},{3,15},{4,0},{5,1},{6,2},{7,3},{8,4},{9,5},{1... | collective-permute-start | bytes 638984 | tf_op jit(solution)/shard_map/ppermute | solution.py:772
  16.5 1.0 collective-permute-start.2
  17.5 4.2 collective-permute-start.3
  21.8 1.3 collective-permute-start.4
  23.0 3.6 all-to-all-start
  26.7 7.8 %collective-permute-done.1 = bf16[64,1664]{1,0:T(8,128)(2,1)S(1)} collective-permute-done((bf16[64,1664]{1,0:T(8,128)(2,1)S(1)}, bf16[64,1664]{1,0:T(8,128)(2,1)S(1)}, u32[]{:S(2)}, u32[]{:S(2)}) %collective-permute-start.1) | collective-permute-done | bytes 213024 | tf_op jit(solution)/shard_map/ppermute | solution.py:772
  34.8 1.0 constant_dynamic-slice_fusion.1.packed
  35.8 10.9 %all-to-all-done = bf16[4,2,96,1024]{3,2,1,0:T(8,128)(2,1)S(1)} async-done(((bf16[4,2,96,1024]{3,2,1,0:T(8,128)(2,1)}), bf16[4,2,96,1024]{3,2,1,0:T(8,128)(2,1)S(1)}, u32[]{:S(2)}, u32[]{:S(2)}) %all-to-all-start) | async-done | bytes 1572896 | tf_op jit(solution)/shard_map/all_to_all | solution.py:803
  46.6 1.1 copy-done.14
  48.1 34.7 %weights_gather.1 = (bf16[4,4,64,2048]{3,2,1,0:T(8,128)(2,1)}, bf16[4,4,64,1024]{3,2,1,0:T(8,128)(2,1)}, bf16[4,4,64,256]{3,2,1,0:T(8,128)(2,1)}) custom-call(bf16[4,64,1664]{2,1,0:T(8,128)(2,1)} %constant_dynamic-slice_fusion.1.packed), custom_call_target="tpu_custom_call" | custom-call | flops 1000000 | bytes 16777216 | tf_op jit(solution)/shard_map/weights_gather/pallas_call | solution.py:376
  82.8 2.0 slice_convert_fusion.2
  85.0 1.2 convert_element_type.159
  86.6 1.0 copy-done.24
  87.6 1.1 copy-done.36
  88.7 1.3 fusion.10
  90.1 0.9 slice.235
  91.5 2.0 copy.87
  93.6 1.2 copy.115
  95.3 2.7 fusion.8
  98.2 1.0 fusion.37
  99.5 0.7 copy-done.22
  100.3 5.3 %fusion.80 = (f32[8,2,256]{2,1,0:T(2,128)S(1)}, f32[8,2,256,512]{2,3,1,0:T(8,128)}) fusion(pred[256,512]{0,1:T(8,128)(4,1)S(1)} %fusion.47, bf16[512,8,64,1]{0,2,3,1:T(8,128)(2,1)S(1)} %fusion.44, bf16[256,8,2,64]{0,3,2,1:T(8,128)(2,1)S(1)} %copy-done.22), kind=kOutput, calls=%fused_computation.190 | convolution fusion | flops 276824576 | bytes 9584640 | tf_op jit(solution)/shard_map/sub | solution.py:860
  105.6 4.4 %fusion.17 = bf16[8,64,2,256]{3,1,2,0:T(8,128)(2,1)S(1)} fusion(bf16[512,8,64,1]{0,2,3,1:T(8,128)(2,1)S(1)} %bitcast.207, f32[8,2,256,512]{2,3,1,0:T(8,128)} %get-tuple-element.130, f32[8,2,256]{2,1,0:T(2,128)S(1)} %get-tuple-element.129), kind=kOutput, calls=%fused_computation.40 | convolution fusion | flops 272891904 | bytes 9453568 | tf_op jit(solution)/shard_map/grqk,kgd->qgrd/dot_general | solution.py:863
  110.0 0.8 multiply_reduce_fusion.5
  112.2 42.9 %group_gather.1 = (bf16[8,256,1024]{2,1,0:T(8,128)(2,1)}, f32[8,16,256]{2,1,0:T(8,128)}, bf16[8,256,1024]{2,1,0:T(8,128)(2,1)}) custom-call(bf16[256,1024]{1,0:T(8,128)(2,1)} %copy-done.15, f32[16,256]{1,0:T(8,128)} %fusion.77.refs_1_, bf16[256,1024]{1,0:T(8,128)(2,1)} %bitcast.211), custom_call_target="tpu_custom_call" | custom-call | flops 1000000000 | bytes 16777216 | tf_op jit(solution)/shard_map/group_gather/pallas_call | solution.py:137
  155.1 1.5 constant_dynamic-slice_fusion.gate_ref
  156.6 5.3 %all-gather.2.cloned.1.call-done.weights_ref = bf16[16,2,96,1024]{3,2,1,0:T(8,128)(2,1)} async-done(((bf16[4,2,96,1024]{3,2,1,0:T(8,128)(2,1)}), bf16[16,2,96,1024]{3,2,1,0:T(8,128)(2,1)}) %all-gather.2.cloned.1.call-update) | async-done | bytes 6291472 | tf_op jit(solution)/shard_map/all_gather | solution.py:824
  161.9 56.2 %expert_layer.1 = (bf16[8,256,1024]{2,1,0:T(8,128)(2,1)}, bf16[8,256,1024]{2,1,0:T(8,128)(2,1)}, f32[8,8,256]{2,1,0:T(8,128)}, bf16[16,2,96,1024]{3,2,1,0:T(8,128)(2,1)}) custom-call(bf16[8,256,1024]{2,1,0:T(8,128)(2,1)} %get-tuple-element.44.rows_ref, bf16[8,256,1024]{2,1,0:T(8,128)(2,1)} %get-tuple-element.45.grad_ref, ...), custom_call_target="tpu_custom_call" | custom-call | flops 44999999488 | bytes 16777216 | tf_op jit(solution)/shard_map/expert_layer/pallas_call | solution.py:696
  218.9 2.2 copy-done.2
  221.1 27.9 %group_reduce.1 = (f32[256,1024]{1,0:T(8,128)S(1)}, f32[8,8,256]{2,1,0:T(8,128)S(1)}) custom-call(bf16[8,256,1024]{2,1,0:T(8,128)(2,1)S(1)} %copy-done.2, f32[8,8,256]{2,1,0:T(8,128)S(1)} %copy-done.4), custom_call_target="tpu_custom_call" | custom-call | flops 1000000 | bytes 16777216 | tf_op jit(solution)/shard_map/group_reduce/pallas_call | solution.py:265
  249.1 2.5 multiply_reduce_fusion.2
  251.6 1.5 subtract_add_fusion
  253.2 1.0 copy-done.7
  254.1 0.8 convolution_convert_fusion.2
  255.2 4.8 %fusion.1 = (f32[8,2,256]{2,1,0:T(2,128)S(1)}, f32[8,512,256,2]{2,1,3,0:T(8,128)S(1)}) fusion(f32[8,2,256,512]{2,3,1,0:T(8,128)} %get-tuple-element.130, f32[8,2,256]{2,1,0:T(2,128)S(1)} %get-tuple-element.129, bf16[512,8,64,1]{0,2,3,1:T(8,128)(2,1)S(1)} %bitcast.208, bf16[256,8,2,64]{0,3,2,1:T(8,128)(2,1)S(1)} %bitcast.209), kind=kOutput, calls=%fused_computation.3 | convolution fusion | flops 274722816 | bytes 17858560 | tf_op jit(solution)/shard_map/qgrd,kgd->grqk/dot_general | solution.py:898
  260.1 0.9 slice-done.1
  261.0 1.5 fusion.3
  262.5 0.8 fusion.21
  263.8 0.8 copy-done.23
  264.5 1.4 fusion.16
  265.9 1.4 fusion.12
  267.4 1.4 collective-permute-start.5
  269.9 12.8 %collective-permute-done.5 = bf16[256,1024]{0,1:T(8,128)(2,1)S(1)} collective-permute-done((bf16[256,1024]{0,1:T(8,128)(2,1)S(1)}, bf16[256,1024]{0,1:T(8,128)(2,1)S(1)}, u32[]{:S(2)}, u32[]{:S(2)}) %collective-permute-start.5) | collective-permute-done | bytes 524320 | tf_op jit(solution)/shard_map/ppermute | solution.py:911
  283.2 2.0 copy-done.37
  285.2 2.4 fusion.29
  287.7 1.1 select_maximum_fusion
  288.8 1.6 copy.97
  290.4 4.6 %convolution_convert_fusion = bf16[1024,2048]{1,0:T(8,128)(2,1)} fusion(bf16[512,1024]{1,0:T(8,128)(2,1)} %copy-done.24, bf16[256,512]{0,1:T(8,128)(2,1)S(1)} %get-tuple-element.114, bf16[256,512]{0,1:T(8,128)(2,1)} %copy-done.30, bf16[256,1024]{0,1:T(8,128)(2,1)} %copy-done.28), kind=kOutput, calls=%fused_computation.14 | convolution fusion | flops 1078984704 | bytes 5767168 | tf_op jit(solution)/shard_map/dot_general | solution.py:919
  294.9 59.3 %weights_reduce.1 = (bf16[4,64,1664]{2,1,0:T(8,128)(2,1)S(1)}, bf16[4,64,1024]{2,1,0:T(8,128)(2,1)S(1)}) custom-call(bf16[4,4,64,2048]{3,2,1,0:T(8,128)(2,1)} %bitcast.196, bf16[4,4,64,1024]{3,2,1,0:T(8,128)(2,1)S(1)} %bitcast.179, f32[4,4,64,256]{3,2,1,0:T(8,128)S(1)} %bitcast.180, bf16[8,4,64,1024]{3,2,1,0:T(8,128)(2,1)} %bitcast.195), custom_call_target="tpu_custom_call" | custom-call | flops 1000000 | bytes 16777216 | tf_op jit(solution)/shard_map/weights_reduce/pallas_call | solution.py:518
  354.3 0.9 multiply_reduce_fusion.1
  355.2 1.6 pad_maximum_fusion.12
  356.8 0.9 fusion.40
  357.7 1.1 fusion.45
  358.9 1.5 collective-permute-done.6
  360.3 1.9 sqrt_bitcast_fusion
  362.2 44.8 %send_pieces.1 = (bf16[8,2,96,1024]{3,2,1,0:T(8,128)(2,1)}, bf16[2,64,1664]{2,1,0:T(8,128)(2,1)}) custom-call(bf16[4,2,96,1024]{3,2,1,0:T(8,128)(2,1)} %reduce-scatter.2.cloned.1.call-done.pieces, bf16[4,64,1664]{2,1,0:T(8,128)(2,1)} %copy-done.3), custom_call_target="tpu_custom_call" | custom-call | tf_op jit(solution)/shard_map/send_pieces/pallas_call | solution.py:598
  407.0 1.8 slice.178
  408.8 1.4 slice.179
  410.9 3.2 convert_bitcast_fusion
  414.1 1.9 convert_bitcast_fusion.1
  416.7 0.7 maximum_convert_fusion.1
  417.5 0.8 maximum_convert_fusion
  (159 shorter events, 9.3 us)
Async XLA Ops:
  7.2 1.5 copy-start
  8.9 2.1 copy-start.38
  8.9 2.1 copy-start.39
  8.9 2.2 copy-start.34
  8.9 2.3 copy-start.31
  9.0 2.3 copy-start.32
  9.0 8.5 %copy-start.10 = (bf16[1,256,1024]{2,1,0:T(8,128)(2,1)S(1)}, bf16[1,256,1024]{2,1,0:T(8,128)(2,1)}, u32[]{:S(2)}) copy-start(bf16[1,256,1024]{2,1,0:T(8,128)(2,1)} %param.11) | copy-start | bytes 1572868
  9.0 12.8 %copy-start.35 = (s32[1,256]{1,0:T(1,128)S(1)}, s32[1,256]{1,0:T(1,128)}, u32[]{:S(2)}) copy-start(s32[1,256]{1,0:T(1,128)} %param.12) | copy-start | bytes 3076
  11.4 15.3 %collective-permute-start = (bf16[64,1664]{1,0:T(8,128)(2,1)S(1)}, bf16[64,1664]{1,0:T(8,128)(2,1)S(1)}, u32[]{:S(2)}, u32[]{:S(2)}) collective-permute-start(bf16[64,1664]{1,0:T(8,128)(2,1)S(1)} %pad_maximum_fusion.8), channel_id=1, source_target_pairs={{0,12},{1,13},{2,14},{3,15},{4,0},{5,1},{6,2},{7,3},{8,4},{9,5},{1... | collective-permute-start | bytes 638984 | tf_op jit(solution)/shard_map/ppermute | solution.py:772
  16.5 18.1 %collective-permute-start.1 = (bf16[64,1664]{1,0:T(8,128)(2,1)S(1)}, bf16[64,1664]{1,0:T(8,128)(2,1)S(1)}, u32[]{:S(2)}, u32[]{:S(2)}) collective-permute-start(bf16[64,1664]{1,0:T(8,128)(2,1)S(1)} %pad_maximum_fusion.8), channel_id=1, source_target_pairs={{0,8},{1,9},{2,10},{3,11},{4,12},{5,13},{6,14},{7,15},{8,0},{9,1},... | collective-permute-start | bytes 638984 | tf_op jit(solution)/shard_map/ppermute | solution.py:772
  16.5 18.1 %collective-permute-start.2 = (bf16[64,1664]{1,0:T(8,128)(2,1)S(1)}, bf16[64,1664]{1,0:T(8,128)(2,1)S(1)}, u32[]{:S(2)}, u32[]{:S(2)}) collective-permute-start(bf16[64,1664]{1,0:T(8,128)(2,1)S(1)} %pad_maximum_fusion.8), channel_id=1, source_target_pairs={{0,4},{1,5},{2,6},{3,7},{4,8},{5,9},{6,10},{7,11},{8,12},{9,13},{1... | collective-permute-start | bytes 638984 | tf_op jit(solution)/shard_map/ppermute | solution.py:772
  17.5 18.2 %collective-permute-start.3 = (bf16[256,1024]{1,0:T(8,128)(2,1)S(1)}, bf16[256,1024]{1,0:T(8,128)(2,1)}, u32[]{:S(2)}, u32[]{:S(2)}) collective-permute-start(bf16[256,1024]{1,0:T(8,128)(2,1)S(1)} %bitcast.187), channel_id=1, source_target_pairs={{0,16},{1,17},{2,18},{3,19},{4,20},{5,21},{6,22},{7,23},{8,24},{9,... | collective-permute-start | bytes 1572872 | tf_op jit(solution)/shard_map/ppermute | solution.py:806
  21.8 14.0 %collective-permute-start.4 = (s32[1,256]{1,0:T(1,128)S(1)}, s32[1,256]{1,0:T(1,128)S(1)}, u32[]{:S(2)}, u32[]{:S(2)}) collective-permute-start(s32[1,256]{1,0:T(1,128)S(1)} %copy-done.35), channel_id=1, source_target_pairs={{0,16},{1,17},{2,18},{3,19},{4,20},{5,21},{6,22},{7,23},{8,24},{9,... | collective-permute-start | bytes 3080 | tf_op jit(solution)/shard_map/ppermute | solution.py:807
  23.0 23.6 %all-to-all-start = ((bf16[4,2,96,1024]{3,2,1,0:T(8,128)(2,1)}), bf16[4,2,96,1024]{3,2,1,0:T(8,128)(2,1)S(1)}, u32[]{:S(2)}, u32[]{:S(2)}) async-start(bf16[4,2,96,1024]{3,2,1,0:T(8,128)(2,1)} %bitcast.190), calls=%async_computation | async-start | bytes 3145728 | tf_op jit(solution)/shard_map/all_to_all | solution.py:803
  26.6 135.2 %all-gather.2.cloned.1.call-start = ((), (), s32[]{:S(2)}) async-start(), calls=%async_computation.2 | async-start | bytes 7864320 | tf_op jit(solution)/shard_map/all_gather | solution.py:824
  34.7 13.2 %copy-start.33 = (s32[1,256,8]{1,2,0:T(8,128)S(1)}, s32[1,256,8]{1,2,0:T(8,128)}, u32[]{:S(2)}) copy-start(s32[1,256,8]{1,2,0:T(8,128)} %param.13) | copy-start | bytes 24580
  46.6 1.1 copy-start.14
  47.8 314.4 %reduce-scatter.2.cloned.1.call-start = ((), (), s32[]{:S(2)}) async-start(), calls=%async_computation.3 | async-start | bytes 7864320 | tf_op jit(solution)/shard_map/reduce_scatter | solution.py:878
  86.1 2.6 copy-start.36
  86.6 1.0 copy-start.24
  99.2 1.0 copy-start.22
  100.3 5.3 %copy-start.17 = (bf16[512,8,64,1]{0,2,3,1:T(8,128)(2,1)}, bf16[512,8,64,1]{0,2,3,1:T(8,128)(2,1)S(1)}, u32[]{:S(2)}) copy-start(bf16[512,8,64,1]{0,2,3,1:T(8,128)(2,1)S(1)} %fusion.44) | copy-start | bytes 1572868
  100.3 5.3 %copy-start.26 = (bf16[512,512]{0,1:T(8,128)(2,1)S(1)}, bf16[512,512]{0,1:T(8,128)(2,1)}, u32[]{:S(2)}) copy-start(bf16[512,512]{0,1:T(8,128)(2,1)} %copy.87) | copy-start | bytes 1572868
  105.6 4.5 %copy-start.12 = (bf16[4,4,64,1024]{3,2,1,0:T(8,128)(2,1)S(1)}, bf16[4,4,64,1024]{3,2,1,0:T(8,128)(2,1)}, u32[]{:S(2)}) copy-start(bf16[4,4,64,1024]{3,2,1,0:T(8,128)(2,1)} %get-tuple-element.43) | copy-start | bytes 6291460
  110.0 0.9 copy-start.19
  110.0 1.2 copy-start.21
  110.9 140.8 %copy-start.5 = (f32[256,1024]{1,0:T(8,128)}, f32[256,1024]{1,0:T(8,128)S(1)}, u32[]{:S(2)}) copy-start(f32[256,1024]{1,0:T(8,128)S(1)} %get-tuple-element.132) | copy-start | bytes 3145732
  111.3 0.9 copy-start.15
  218.1 0.8 copy-start.4
  218.9 2.2 copy-start.2
  251.6 2.5 copy-start.13
  253.2 1.0 copy-start.7
  254.1 1.0 copy-start.27
  255.1 4.9 %slice-start = ((s8[8388608]{0:T(1024)(128)(4,1)}), s8[4194304]{0:T(1024)(128)(4,1)S(1)}, s32[]{:S(2)}) async-start(s8[8388608]{0:T(1024)(128)(4,1)} %bitcast.185), calls=%async_computation.4 | async-start | bytes 8388608
  255.2 5.8 %slice-start.1 = ((s8[8388608]{0:T(1024)(128)(4,1)}), s8[4194304]{0:T(1024)(128)(4,1)S(1)}, s32[]{:S(2)}) async-start(s8[8388608]{0:T(1024)(128)(4,1)} %bitcast.185), calls=%async_computation.5 | async-start | bytes 8388608
  261.0 1.5 copy-start.18
  263.5 1.0 copy-start.23
  264.5 18.7 %copy-start.28 = (bf16[256,1024]{0,1:T(8,128)(2,1)}, bf16[256,1024]{0,1:T(8,128)(2,1)S(1)}, u32[]{:S(2)}) copy-start(bf16[256,1024]{0,1:T(8,128)(2,1)S(1)} %fusion.39) | copy-start | bytes 1572868
  267.3 1.5 copy-start.16
  267.3 1.9 copy-start.8
  267.3 1.9 copy-start.20
  267.4 15.3 %collective-permute-start.5 = (bf16[256,1024]{0,1:T(8,128)(2,1)S(1)}, bf16[256,1024]{0,1:T(8,128)(2,1)S(1)}, u32[]{:S(2)}, u32[]{:S(2)}) collective-permute-start(bf16[256,1024]{0,1:T(8,128)(2,1)S(1)} %fusion.33), channel_id=1, source_target_pairs={{16,0},{17,1},{18,2},{19,3},{20,4},{21,5},{22,6},{23,7},{24,8},{25... | collective-permute-start | bytes 1572872 | tf_op jit(solution)/shard_map/ppermute | solution.py:911
  283.0 2.3 copy-start.37
  283.2 4.5 %copy-start.30 = (bf16[256,512]{0,1:T(8,128)(2,1)}, bf16[256,512]{0,1:T(8,128)(2,1)S(1)}, u32[]{:S(2)}) copy-start(bf16[256,512]{0,1:T(8,128)(2,1)S(1)} %fusion.46) | copy-start | bytes 786436
  294.9 61.8 %copy-start.6 = (f32[256,1024]{1,0:T(8,128)S(1)}, f32[256,1024]{1,0:T(8,128)}, u32[]{:S(2)}) copy-start(f32[256,1024]{1,0:T(8,128)} %copy-done.5) | copy-start | bytes 3145732
  354.3 4.6 %copy-start.3 = (bf16[4,64,1664]{2,1,0:T(8,128)(2,1)}, bf16[4,64,1664]{2,1,0:T(8,128)(2,1)S(1)}, u32[]{:S(2)}) copy-start(bf16[4,64,1664]{2,1,0:T(8,128)(2,1)S(1)} %get-tuple-element.55.packed) | copy-start | bytes 2555908
  354.3 3.4 copy-start.9
  354.3 3.4 copy-start.11
  354.3 3.4 copy-start.25
  356.7 3.6 collective-permute-start.6
  408.7 1.4 copy-start.29
  410.9 7.4 %copy-start.1 = (bf16[32,16,1024]{2,1,0:T(8,128)(2,1)S(1)}, bf16[32,16,1024]{2,1,0:T(8,128)(2,1)}, u32[]{:S(2)}) copy-start(bf16[32,16,1024]{2,1,0:T(8,128)(2,1)} %param.20) | copy-start | bytes 3145732
Sparse Core Ops, SparseCore 0:
  47.9 113.8 all-gather.1
  218.2 108.9 reduce-scatter.1

commit v2 on v1

--- a/solution.py
+++ b/solution.py
@@ -153,12 +153,14 @@
 
 
 def add_rows(target, source, start, size):
+    chunk = 32 if size % 32 == 0 else 16
+
     def step(i, carry):
-        rows = pl.ds(pl.multiple_of(start + i * 16, 16), 16)
+        rows = pl.ds(pl.multiple_of(start + i * chunk, chunk), chunk)
         target[rows] = (target[rows].astype(f32) + source[rows].astype(f32)).astype(target.dtype)
         return carry
 
-    lax.fori_loop(0, size // 16, step, 0)
+    lax.fori_loop(0, size // chunk, step, 0)
 
 
 def reduce_kernel(
@@ -393,10 +395,11 @@
 def add_block(target, source, at, start, size):
     groups, rows = source.shape[0], source.shape[1]
     columns = pl.ds(start, size)
-    pieces = rows // 16
+    chunk = 64 if rows % 64 == 0 else 16
+    pieces = rows // chunk
 
     def step(i, carry):
-        lines = pl.ds(pl.multiple_of((i % pieces) * 16, 16), 16)
+        lines = pl.ds(pl.multiple_of((i % pieces) * chunk, chunk), chunk)
         index = (i // pieces, lines, columns)
         new = target[(at,) + index].astype(f32) + source[index].astype(f32)
         target[(at,) + index] = new.astype(target.dtype)

time: 426 us -> 425 us (level)
  no operation moved by 1% of the time
where the time goes in v2:
time: 425 us; the launch traced here: 423 us
  Pallas kernels  264 us (62%)
  waiting for transfers between devices  38.3 us (9%)
  matrix products  34.5 us (8%)
  local copies, waits for them, and re-layouts  29.4 us (7%)
  other arithmetic  25.3 us (6%)
  starting transfers between devices  16.8 us (4%)
  between operations  15 us (4%)
    pallas_call x1, Pallas kernels, weights_reduce(): pl.pallas_call(functools.partial(weights_reduce_kernel, count), out_shape...  58 us
    pallas_call x1, Pallas kernels, expert_layer(): pl.pallas_call(functools.partial(expert_kernel, first), grid=(GROUP // sh...  56.2 us
    pallas_call x1, Pallas kernels, send_pieces(): pl.pallas_call(pieces_kernel, out_shape=[jax.ShapeDtypeStruct((GROUP,) +...  44.6 us
    pallas_call x1, Pallas kernels, group_gather(): pl.pallas_call(functools.partial(gather_kernel, count), out_shape=[jax.Sh...  42.9 us
    pallas_call x1, Pallas kernels, weights_gather(): pl.pallas_call(functools.partial(weights_gather_kernel, halves), out_shap...  34.7 us
    pallas_call x1, Pallas kernels, group_reduce(): pl.pallas_call(reduce_kernel, out_shape=[jax.ShapeDtypeStruct((rows, widt...  27.8 us
    unnamed x93, local copies, waits for them, and re-layouts  14.4 us
    ppermute x1, waiting for transfers between devices, body(): kv_back = lax.ppermute(kv_grad[:count].astype(bf16), 'seq', back_pair)  12.8 us
  transfers between devices with their start and end apart: 10, of which 5 were waited for; matrix products, arithmetic and copies ran while one was open for 15% of the time, Pallas kernels for 39%

profile of v2, /device:TPU:0, one launch (start us, length us, event | category | flops | bytes accessed | tf_op | source)
XLA Modules:
  0.0 423.5 jit_solution(1219403105561872598)
XLA Ops:
  7.2 1.4 dynamic-slice_bitcast_fusion
  9.0 2.0 copy.83
  11.4 5.1 %collective-permute-start = (bf16[64,1664]{1,0:T(8,128)(2,1)S(1)}, bf16[64,1664]{1,0:T(8,128)(2,1)S(1)}, u32[]{:S(2)}, u32[]{:S(2)}) collective-permute-start(bf16[64,1664]{1,0:T(8,128)(2,1)S(1)} %pad_maximum_fusion.8), channel_id=1, source_target_pairs={{0,12},{1,13},{2,14},{3,15},{4,0},{5,1},{6,2},{7,3},{8,4},{9,5},{1... | collective-permute-start | bytes 638984 | tf_op jit(solution)/shard_map/ppermute | solution.py:775
  16.5 1.0 collective-permute-start.2
  17.5 4.2 %collective-permute-start.3 = (bf16[256,1024]{1,0:T(8,128)(2,1)S(1)}, bf16[256,1024]{1,0:T(8,128)(2,1)}, u32[]{:S(2)}, u32[]{:S(2)}) collective-permute-start(bf16[256,1024]{1,0:T(8,128)(2,1)S(1)} %bitcast.187), channel_id=1, source_target_pairs={{0,16},{1,17},{2,18},{3,19},{4,20},{5,21},{6,22},{7,23},{8,24},{9,... | collective-permute-start | bytes 1572872 | tf_op jit(solution)/shard_map/ppermute | solution.py:809
  21.8 1.3 collective-permute-start.4
  23.0 3.6 all-to-all-start
  26.7 7.8 %collective-permute-done.1 = bf16[64,1664]{1,0:T(8,128)(2,1)S(1)} collective-permute-done((bf16[64,1664]{1,0:T(8,128)(2,1)S(1)}, bf16[64,1664]{1,0:T(8,128)(2,1)S(1)}, u32[]{:S(2)}, u32[]{:S(2)}) %collective-permute-start.1) | collective-permute-done | bytes 213024 | tf_op jit(solution)/shard_map/ppermute | solution.py:775
  34.8 1.0 constant_dynamic-slice_fusion.1.packed
  35.8 10.9 %all-to-all-done = bf16[4,2,96,1024]{3,2,1,0:T(8,128)(2,1)S(1)} async-done(((bf16[4,2,96,1024]{3,2,1,0:T(8,128)(2,1)}), bf16[4,2,96,1024]{3,2,1,0:T(8,128)(2,1)S(1)}, u32[]{:S(2)}, u32[]{:S(2)}) %all-to-all-start) | async-done | bytes 1572896 | tf_op jit(solution)/shard_map/all_to_all | solution.py:806
  46.6 1.1 copy-done.14
  48.1 34.7 %weights_gather.1 = (bf16[4,4,64,2048]{3,2,1,0:T(8,128)(2,1)}, bf16[4,4,64,1024]{3,2,1,0:T(8,128)(2,1)}, bf16[4,4,64,256]{3,2,1,0:T(8,128)(2,1)}) custom-call(bf16[4,64,1664]{2,1,0:T(8,128)(2,1)} %constant_dynamic-slice_fusion.1.packed), custom_call_target="tpu_custom_call" | custom-call | flops 1000000 | bytes 16777216 | tf_op jit(solution)/shard_map/weights_gather/pallas_call | solution.py:378
  82.8 2.0 slice_convert_fusion.2
  85.0 1.2 convert_element_type.159
  86.6 1.0 copy-done.24
  87.6 1.1 copy-done.36
  88.7 1.3 fusion.10
  90.1 0.9 slice.235
  91.5 2.0 copy.87
  93.6 1.2 copy.115
  95.3 2.7 fusion.8
  98.2 1.0 fusion.37
  99.5 0.7 copy-done.22
  100.3 5.3 %fusion.80 = (f32[8,2,256]{2,1,0:T(2,128)S(1)}, f32[8,2,256,512]{2,3,1,0:T(8,128)}) fusion(pred[256,512]{0,1:T(8,128)(4,1)S(1)} %fusion.47, bf16[512,8,64,1]{0,2,3,1:T(8,128)(2,1)S(1)} %fusion.44, bf16[256,8,2,64]{0,3,2,1:T(8,128)(2,1)S(1)} %copy-done.22), kind=kOutput, calls=%fused_computation.190 | convolution fusion | flops 276824576 | bytes 9584640 | tf_op jit(solution)/shard_map/sub | solution.py:863
  105.6 4.4 %fusion.17 = bf16[8,64,2,256]{3,1,2,0:T(8,128)(2,1)S(1)} fusion(bf16[512,8,64,1]{0,2,3,1:T(8,128)(2,1)S(1)} %bitcast.207, f32[8,2,256,512]{2,3,1,0:T(8,128)} %get-tuple-element.130, f32[8,2,256]{2,1,0:T(2,128)S(1)} %get-tuple-element.129), kind=kOutput, calls=%fused_computation.40 | convolution fusion | flops 272891904 | bytes 9453568 | tf_op jit(solution)/shard_map/grqk,kgd->qgrd/dot_general | solution.py:866
  110.0 0.8 multiply_reduce_fusion.5
  112.2 42.9 %group_gather.1 = (bf16[8,256,1024]{2,1,0:T(8,128)(2,1)}, f32[8,16,256]{2,1,0:T(8,128)}, bf16[8,256,1024]{2,1,0:T(8,128)(2,1)}) custom-call(bf16[256,1024]{1,0:T(8,128)(2,1)} %copy-done.15, f32[16,256]{1,0:T(8,128)} %fusion.77.refs_1_, bf16[256,1024]{1,0:T(8,128)(2,1)} %bitcast.211), custom_call_target="tpu_custom_call" | custom-call | flops 1000000000 | bytes 16777216 | tf_op jit(solution)/shard_map/group_gather/pallas_call | solution.py:137
  155.1 1.5 constant_dynamic-slice_fusion.gate_ref
  156.6 5.3 %all-gather.2.cloned.1.call-done.weights_ref = bf16[16,2,96,1024]{3,2,1,0:T(8,128)(2,1)} async-done(((bf16[4,2,96,1024]{3,2,1,0:T(8,128)(2,1)}), bf16[16,2,96,1024]{3,2,1,0:T(8,128)(2,1)}) %all-gather.2.cloned.1.call-update) | async-done | bytes 6291472 | tf_op jit(solution)/shard_map/all_gather | solution.py:827
  161.9 56.2 %expert_layer.1 = (bf16[8,256,1024]{2,1,0:T(8,128)(2,1)}, bf16[8,256,1024]{2,1,0:T(8,128)(2,1)}, f32[8,8,256]{2,1,0:T(8,128)}, bf16[16,2,96,1024]{3,2,1,0:T(8,128)(2,1)}) custom-call(bf16[8,256,1024]{2,1,0:T(8,128)(2,1)} %get-tuple-element.44.rows_ref, bf16[8,256,1024]{2,1,0:T(8,128)(2,1)} %get-tuple-element.45.grad_ref, ...), custom_call_target="tpu_custom_call" | custom-call | flops 44999999488 | bytes 16777216 | tf_op jit(solution)/shard_map/expert_layer/pallas_call | solution.py:699
  218.9 2.2 copy-done.2
  221.1 27.8 %group_reduce.1 = (f32[256,1024]{1,0:T(8,128)S(1)}, f32[8,8,256]{2,1,0:T(8,128)S(1)}) custom-call(bf16[8,256,1024]{2,1,0:T(8,128)(2,1)S(1)} %copy-done.2, f32[8,8,256]{2,1,0:T(8,128)S(1)} %copy-done.4), custom_call_target="tpu_custom_call" | custom-call | flops 1000000 | bytes 16777216 | tf_op jit(solution)/shard_map/group_reduce/pallas_call | solution.py:267
  248.9 2.5 multiply_reduce_fusion.2
  251.5 1.5 subtract_add_fusion
  253.0 1.0 copy-done.7
  254.0 0.8 convolution_convert_fusion.2
  255.0 4.8 %fusion.1 = (f32[8,2,256]{2,1,0:T(2,128)S(1)}, f32[8,512,256,2]{2,1,3,0:T(8,128)S(1)}) fusion(f32[8,2,256,512]{2,3,1,0:T(8,128)} %get-tuple-element.130, f32[8,2,256]{2,1,0:T(2,128)S(1)} %get-tuple-element.129, bf16[512,8,64,1]{0,2,3,1:T(8,128)(2,1)S(1)} %bitcast.208, bf16[256,8,2,64]{0,3,2,1:T(8,128)(2,1)S(1)} %bitcast.209), kind=kOutput, calls=%fused_computation.3 | convolution fusion | flops 274722816 | bytes 17858560 | tf_op jit(solution)/shard_map/qgrd,kgd->grqk/dot_general | solution.py:901
  259.9 0.9 slice-done.1
  260.8 1.5 fusion.3
  262.4 0.8 fusion.21
  263.6 0.8 copy-done.23
  264.4 1.4 fusion.16
  265.8 1.4 fusion.12
  267.3 1.4 collective-permute-start.5
  269.8 12.8 %collective-permute-done.5 = bf16[256,1024]{0,1:T(8,128)(2,1)S(1)} collective-permute-done((bf16[256,1024]{0,1:T(8,128)(2,1)S(1)}, bf16[256,1024]{0,1:T(8,128)(2,1)S(1)}, u32[]{:S(2)}, u32[]{:S(2)}) %collective-permute-start.5) | collective-permute-done | bytes 524320 | tf_op jit(solution)/shard_map/ppermute | solution.py:914
  283.1 2.0 copy-done.37
  285.1 2.4 fusion.29
  287.6 1.1 select_maximum_fusion
  288.6 1.6 copy.97
  290.2 4.6 %convolution_convert_fusion = bf16[1024,2048]{1,0:T(8,128)(2,1)} fusion(bf16[512,1024]{1,0:T(8,128)(2,1)} %copy-done.24, bf16[256,512]{0,1:T(8,128)(2,1)S(1)} %get-tuple-element.114, bf16[256,512]{0,1:T(8,128)(2,1)} %copy-done.30, bf16[256,1024]{0,1:T(8,128)(2,1)} %copy-done.28), kind=kOutput, calls=%fused_computation.14 | convolution fusion | flops 1078984704 | bytes 5767168 | tf_op jit(solution)/shard_map/dot_general | solution.py:922
  294.8 58.0 %weights_reduce.1 = (bf16[4,64,1664]{2,1,0:T(8,128)(2,1)S(1)}, bf16[4,64,1024]{2,1,0:T(8,128)(2,1)S(1)}) custom-call(bf16[4,4,64,2048]{3,2,1,0:T(8,128)(2,1)} %bitcast.196, bf16[4,4,64,1024]{3,2,1,0:T(8,128)(2,1)S(1)} %bitcast.179, f32[4,4,64,256]{3,2,1,0:T(8,128)S(1)} %bitcast.180, bf16[8,4,64,1024]{3,2,1,0:T(8,128)(2,1)} %bitcast.195), custom_call_target="tpu_custom_call" | custom-call | flops 1000000 | bytes 16777216 | tf_op jit(solution)/shard_map/weights_reduce/pallas_call | solution.py:521
  352.8 0.9 multiply_reduce_fusion.1
  353.7 1.6 pad_maximum_fusion.12
  355.3 0.9 fusion.40
  356.3 1.1 fusion.45
  357.4 1.5 collective-permute-done.6
  358.8 1.9 sqrt_bitcast_fusion
  360.7 44.6 %send_pieces.1 = (bf16[8,2,96,1024]{3,2,1,0:T(8,128)(2,1)}, bf16[2,64,1664]{2,1,0:T(8,128)(2,1)}) custom-call(bf16[4,2,96,1024]{3,2,1,0:T(8,128)(2,1)} %reduce-scatter.2.cloned.1.call-done.pieces, bf16[4,64,1664]{2,1,0:T(8,128)(2,1)} %copy-done.3), custom_call_target="tpu_custom_call" | custom-call | tf_op jit(solution)/shard_map/send_pieces/pallas_call | solution.py:601
  405.3 1.8 slice.178
  407.1 1.4 slice.179
  409.3 3.2 convert_bitcast_fusion
  412.5 1.9 convert_bitcast_fusion.1
  415.1 0.7 maximum_convert_fusion.1
  415.8 0.8 maximum_convert_fusion
  (159 shorter events, 9.3 us)
Async XLA Ops:
  7.2 1.5 copy-start
  8.9 2.1 copy-start.38
  8.9 2.1 copy-start.39
  8.9 2.2 copy-start.34
  8.9 2.3 copy-start.31
  9.0 2.3 copy-start.32
  9.0 8.5 %copy-start.10 = (bf16[1,256,1024]{2,1,0:T(8,128)(2,1)S(1)}, bf16[1,256,1024]{2,1,0:T(8,128)(2,1)}, u32[]{:S(2)}) copy-start(bf16[1,256,1024]{2,1,0:T(8,128)(2,1)} %param.11) | copy-start | bytes 1572868
  9.0 12.8 %copy-start.35 = (s32[1,256]{1,0:T(1,128)S(1)}, s32[1,256]{1,0:T(1,128)}, u32[]{:S(2)}) copy-start(s32[1,256]{1,0:T(1,128)} %param.12) | copy-start | bytes 3076
  11.4 15.3 %collective-permute-start = (bf16[64,1664]{1,0:T(8,128)(2,1)S(1)}, bf16[64,1664]{1,0:T(8,128)(2,1)S(1)}, u32[]{:S(2)}, u32[]{:S(2)}) collective-permute-start(bf16[64,1664]{1,0:T(8,128)(2,1)S(1)} %pad_maximum_fusion.8), channel_id=1, source_target_pairs={{0,12},{1,13},{2,14},{3,15},{4,0},{5,1},{6,2},{7,3},{8,4},{9,5},{1... | collective-permute-start | bytes 638984 | tf_op jit(solution)/shard_map/ppermute | solution.py:775
  16.5 18.1 %collective-permute-start.1 = (bf16[64,1664]{1,0:T(8,128)(2,1)S(1)}, bf16[64,1664]{1,0:T(8,128)(2,1)S(1)}, u32[]{:S(2)}, u32[]{:S(2)}) collective-permute-start(bf16[64,1664]{1,0:T(8,128)(2,1)S(1)} %pad_maximum_fusion.8), channel_id=1, source_target_pairs={{0,8},{1,9},{2,10},{3,11},{4,12},{5,13},{6,14},{7,15},{8,0},{9,1},... | collective-permute-start | bytes 638984 | tf_op jit(solution)/shard_map/ppermute | solution.py:775
  16.5 18.1 %collective-permute-start.2 = (bf16[64,1664]{1,0:T(8,128)(2,1)S(1)}, bf16[64,1664]{1,0:T(8,128)(2,1)S(1)}, u32[]{:S(2)}, u32[]{:S(2)}) collective-permute-start(bf16[64,1664]{1,0:T(8,128)(2,1)S(1)} %pad_maximum_fusion.8), channel_id=1, source_target_pairs={{0,4},{1,5},{2,6},{3,7},{4,8},{5,9},{6,10},{7,11},{8,12},{9,13},{1... | collective-permute-start | bytes 638984 | tf_op jit(solution)/shard_map/ppermute | solution.py:775
  17.5 18.2 %collective-permute-start.3 = (bf16[256,1024]{1,0:T(8,128)(2,1)S(1)}, bf16[256,1024]{1,0:T(8,128)(2,1)}, u32[]{:S(2)}, u32[]{:S(2)}) collective-permute-start(bf16[256,1024]{1,0:T(8,128)(2,1)S(1)} %bitcast.187), channel_id=1, source_target_pairs={{0,16},{1,17},{2,18},{3,19},{4,20},{5,21},{6,22},{7,23},{8,24},{9,... | collective-permute-start | bytes 1572872 | tf_op jit(solution)/shard_map/ppermute | solution.py:809
  21.8 14.0 %collective-permute-start.4 = (s32[1,256]{1,0:T(1,128)S(1)}, s32[1,256]{1,0:T(1,128)S(1)}, u32[]{:S(2)}, u32[]{:S(2)}) collective-permute-start(s32[1,256]{1,0:T(1,128)S(1)} %copy-done.35), channel_id=1, source_target_pairs={{0,16},{1,17},{2,18},{3,19},{4,20},{5,21},{6,22},{7,23},{8,24},{9,... | collective-permute-start | bytes 3080 | tf_op jit(solution)/shard_map/ppermute | solution.py:810
  23.0 23.6 %all-to-all-start = ((bf16[4,2,96,1024]{3,2,1,0:T(8,128)(2,1)}), bf16[4,2,96,1024]{3,2,1,0:T(8,128)(2,1)S(1)}, u32[]{:S(2)}, u32[]{:S(2)}) async-start(bf16[4,2,96,1024]{3,2,1,0:T(8,128)(2,1)} %bitcast.190), calls=%async_computation | async-start | bytes 3145728 | tf_op jit(solution)/shard_map/all_to_all | solution.py:806
  26.6 135.2 %all-gather.2.cloned.1.call-start = ((), (), s32[]{:S(2)}) async-start(), calls=%async_computation.2 | async-start | bytes 7864320 | tf_op jit(solution)/shard_map/all_gather | solution.py:827
  34.7 13.2 %copy-start.33 = (s32[1,256,8]{1,2,0:T(8,128)S(1)}, s32[1,256,8]{1,2,0:T(8,128)}, u32[]{:S(2)}) copy-start(s32[1,256,8]{1,2,0:T(8,128)} %param.13) | copy-start | bytes 24580
  46.6 1.1 copy-start.14
  47.8 312.9 %reduce-scatter.2.cloned.1.call-start = ((), (), s32[]{:S(2)}) async-start(), calls=%async_computation.3 | async-start | bytes 7864320 | tf_op jit(solution)/shard_map/reduce_scatter | solution.py:881
  86.1 2.6 copy-start.36
  86.6 1.0 copy-start.24
  99.2 1.0 copy-start.22
  100.3 5.3 %copy-start.17 = (bf16[512,8,64,1]{0,2,3,1:T(8,128)(2,1)}, bf16[512,8,64,1]{0,2,3,1:T(8,128)(2,1)S(1)}, u32[]{:S(2)}) copy-start(bf16[512,8,64,1]{0,2,3,1:T(8,128)(2,1)S(1)} %fusion.44) | copy-start | bytes 1572868
  100.3 5.3 %copy-start.26 = (bf16[512,512]{0,1:T(8,128)(2,1)S(1)}, bf16[512,512]{0,1:T(8,128)(2,1)}, u32[]{:S(2)}) copy-start(bf16[512,512]{0,1:T(8,128)(2,1)} %copy.87) | copy-start | bytes 1572868
  105.6 4.5 %copy-start.12 = (bf16[4,4,64,1024]{3,2,1,0:T(8,128)(2,1)S(1)}, bf16[4,4,64,1024]{3,2,1,0:T(8,128)(2,1)}, u32[]{:S(2)}) copy-start(bf16[4,4,64,1024]{3,2,1,0:T(8,128)(2,1)} %get-tuple-element.43) | copy-start | bytes 6291460
  110.0 0.9 copy-start.19
  110.0 1.2 copy-start.21
  110.9 140.6 %copy-start.5 = (f32[256,1024]{1,0:T(8,128)}, f32[256,1024]{1,0:T(8,128)S(1)}, u32[]{:S(2)}) copy-start(f32[256,1024]{1,0:T(8,128)S(1)} %get-tuple-element.132) | copy-start | bytes 3145732
  111.3 0.9 copy-start.15
  218.1 0.8 copy-start.4
  218.9 2.2 copy-start.2
  251.5 2.5 copy-start.13
  253.0 1.0 copy-start.7
  254.0 1.0 copy-start.27
  255.0 4.9 %slice-start = ((s8[8388608]{0:T(1024)(128)(4,1)}), s8[4194304]{0:T(1024)(128)(4,1)S(1)}, s32[]{:S(2)}) async-start(s8[8388608]{0:T(1024)(128)(4,1)} %bitcast.185), calls=%async_computation.4 | async-start | bytes 8388608
  255.0 5.8 %slice-start.1 = ((s8[8388608]{0:T(1024)(128)(4,1)}), s8[4194304]{0:T(1024)(128)(4,1)S(1)}, s32[]{:S(2)}) async-start(s8[8388608]{0:T(1024)(128)(4,1)} %bitcast.185), calls=%async_computation.5 | async-start | bytes 8388608
  260.8 1.5 copy-start.18
  263.3 1.0 copy-start.23
  264.4 18.7 %copy-start.28 = (bf16[256,1024]{0,1:T(8,128)(2,1)}, bf16[256,1024]{0,1:T(8,128)(2,1)S(1)}, u32[]{:S(2)}) copy-start(bf16[256,1024]{0,1:T(8,128)(2,1)S(1)} %fusion.39) | copy-start | bytes 1572868
  267.2 1.5 copy-start.16
  267.2 1.9 copy-start.8
  267.2 1.9 copy-start.20
  267.3 15.3 %collective-permute-start.5 = (bf16[256,1024]{0,1:T(8,128)(2,1)S(1)}, bf16[256,1024]{0,1:T(8,128)(2,1)S(1)}, u32[]{:S(2)}, u32[]{:S(2)}) collective-permute-start(bf16[256,1024]{0,1:T(8,128)(2,1)S(1)} %fusion.33), channel_id=1, source_target_pairs={{16,0},{17,1},{18,2},{19,3},{20,4},{21,5},{22,6},{23,7},{24,8},{25... | collective-permute-start | bytes 1572872 | tf_op jit(solution)/shard_map/ppermute | solution.py:914
  282.8 2.3 copy-start.37
  283.1 4.5 %copy-start.30 = (bf16[256,512]{0,1:T(8,128)(2,1)}, bf16[256,512]{0,1:T(8,128)(2,1)S(1)}, u32[]{:S(2)}) copy-start(bf16[256,512]{0,1:T(8,128)(2,1)S(1)} %fusion.46) | copy-start | bytes 786436
  294.8 60.5 %copy-start.6 = (f32[256,1024]{1,0:T(8,128)S(1)}, f32[256,1024]{1,0:T(8,128)}, u32[]{:S(2)}) copy-start(f32[256,1024]{1,0:T(8,128)} %copy-done.5) | copy-start | bytes 3145732
  352.8 4.6 %copy-start.3 = (bf16[4,64,1664]{2,1,0:T(8,128)(2,1)}, bf16[4,64,1664]{2,1,0:T(8,128)(2,1)S(1)}, u32[]{:S(2)}) copy-start(bf16[4,64,1664]{2,1,0:T(8,128)(2,1)S(1)} %get-tuple-element.55.packed) | copy-start | bytes 2555908
  352.8 3.4 copy-start.9
  352.8 3.4 copy-start.11
  352.8 3.4 copy-start.25
  355.3 3.6 collective-permute-start.6
  407.1 1.4 copy-start.29
  409.3 7.4 %copy-start.1 = (bf16[32,16,1024]{2,1,0:T(8,128)(2,1)S(1)}, bf16[32,16,1024]{2,1,0:T(8,128)(2,1)}, u32[]{:S(2)}) copy-start(bf16[32,16,1024]{2,1,0:T(8,128)(2,1)} %param.20) | copy-start | bytes 3145732
Sparse Core Ops, SparseCore 0:
  47.9 113.8 all-gather.1
  218.2 108.9 reduce-scatter.1

commit v3 on v2

--- a/solution.py
+++ b/solution.py
@@ -918,10 +918,15 @@
         key_back = unrotate(
             kv_grad[:, :key_columns].reshape(count, KEY_VALUE_HEADS, HEAD_SIZE), cosine, sine
         ).reshape(count, key_columns)
-        projected_grad = jnp.concatenate([query_back, key_back, kv_grad[:, key_columns:]], 1).astype(bf16)
-        qkv_wgrad = lax.dot_general(normed_one, projected_grad, over_rows, preferred_element_type=f32)
+        query_projected = query_back.astype(bf16)
+        kv_projected = jnp.concatenate([key_back, kv_grad[:, key_columns:]], 1).astype(bf16)
+        query_wgrad = lax.dot_general(normed_one, query_projected, over_rows, preferred_element_type=f32)
+        kv_wgrad = lax.dot_general(normed_one, kv_projected, over_rows, preferred_element_type=f32)
+        over_columns = (((1,), (1,)), ((), ()))
         normed_one_grad = lax.dot_general(
-            projected_grad, qkv_weight, (((1,), (1,)), ((), ())), preferred_element_type=f32
+            query_projected, qkv_weight[:, :query_columns], over_columns, preferred_element_type=f32
+        ) + lax.dot_general(
+            kv_projected, qkv_weight[:, query_columns:], over_columns, preferred_element_type=f32
         )
         rows_branch, gain_one_grad = norm_back(token_rows, gain_a, normed_one_grad)
         input_grad = (hidden_grad + rows_branch).astype(bf16)[None]
@@ -930,17 +935,20 @@
             [spare(router_wgrad), spare(jnp.stack([gain_one_grad, gain_two_grad], 1))], 1
         )
         packed, mixed = weights_reduce(
-            3, expert_groups, (qkv_wgrad.astype(bf16), out_wgrad.astype(bf16), little), mixed_part
+            3, expert_groups,
+            (query_wgrad.astype(bf16), kv_wgrad.astype(bf16), out_wgrad.astype(bf16), little), mixed_part
         )
         mixed = mixed.reshape(count, MODEL_WIDTH).astype(f32)
         output = (hidden + mixed).astype(bf16)[None]
         stat_sums = jnp.stack([jnp.sum(hidden * hidden), jnp.sum(mixed * mixed)])
         stat_sums = stat_sums + lax.ppermute(stat_sums, "seq", [(0, 1), (1, 0)])
         experts_all, ends = send_pieces(4, expert_grads, packed)
-        qkv_shard, out_shard, little = [
+        widths = [query_columns // 2, key_columns, MODEL_WIDTH // 2, 128]
+        query_shard, kv_shard, out_shard, little = [
             jnp.concatenate([ends[0, :, f : f + h], ends[1, :, f : f + h]], 1).astype(f32)
-            for f, h in zip(starts_of(halves), halves)
+            for f, h in zip(starts_of(widths), widths)
         ]
+        qkv_shard = jnp.concatenate([query_shard, kv_shard], 1)
         experts_all = experts_all.reshape((EXPERTS,) + experts_all.shape[2:])
         first = w_gate_up.shape[0]
         stream_rms = jnp.sqrt(stat_sums / (both * MODEL_WIDTH)).reshape(1, 2)

time: 425 us -> 426 us (level); the launches traced: 423 us -> 419 us
  waiting for transfers between devices: 38.3 us -> 32.5 us
    ppermute x1, waiting for transfers between devices: 12.8 us -> 8.23 us  [body(): kv_back = lax.ppermute(kv_grad[:count].astype(bf16), 'seq', back_pair)]
    unnamed x93 -> x89, local copies, waits for them, and re-layouts: 14.4 us -> 11.8 us
  transfers between devices with their start and end apart: 10 -> 10, of which waited for: 5 -> 5; matrix products, arithmetic and copies ran while one was open for 15% -> 16% of each run, Pallas kernels for 39% -> 39%
where the time goes in v3:
time: 426 us; the launch traced here: 419 us
  Pallas kernels  263 us (62%)
  matrix products  37.7 us (9%)
  waiting for transfers between devices  32.5 us (8%)
  local copies, waits for them, and re-layouts  26.8 us (6%)
  other arithmetic  26.3 us (6%)
  starting transfers between devices  17.1 us (4%)
  between operations  15.5 us (4%)
    pallas_call x1, Pallas kernels, weights_reduce(): pl.pallas_call(functools.partial(weights_reduce_kernel, count), out_shape...  57.7 us
    pallas_call x1, Pallas kernels, expert_layer(): pl.pallas_call(functools.partial(expert_kernel, first), grid=(GROUP // sh...  56.2 us
    pallas_call x1, Pallas kernels, send_pieces(): pl.pallas_call(pieces_kernel, out_shape=[jax.ShapeDtypeStruct((GROUP,) +...  44 us
    pallas_call x1, Pallas kernels, group_gather(): pl.pallas_call(functools.partial(gather_kernel, count), out_shape=[jax.Sh...  43 us
    pallas_call x1, Pallas kernels, weights_gather(): pl.pallas_call(functools.partial(weights_gather_kernel, halves), out_shap...  34.7 us
    pallas_call x1, Pallas kernels, group_reduce(): pl.pallas_call(reduce_kernel, out_shape=[jax.ShapeDtypeStruct((rows, widt...  27.8 us
    unnamed x89, local copies, waits for them, and re-layouts  11.8 us
    all_to_all x1, waiting for transfers between devices, body(): lax.all_to_all(mine, 'dp', split_axis=0, concat_axis=0, tiled=True, axis_...  10.9 us
  transfers between devices with their start and end apart: 10, of which 5 were waited for; matrix products, arithmetic and copies ran while one was open for 16% of the time, Pallas kernels for 39%

profile of v3, /device:TPU:0, one launch (start us, length us, event | category | flops | bytes accessed | tf_op | source)
XLA Modules:
  0.0 419.3 jit_solution(13140668804503226364)
XLA Ops:
  7.2 1.4 dynamic-slice_bitcast_fusion
  9.0 2.0 copy.83
  11.4 5.1 %collective-permute-start = (bf16[64,1664]{1,0:T(8,128)(2,1)S(1)}, bf16[64,1664]{1,0:T(8,128)(2,1)S(1)}, u32[]{:S(2)}, u32[]{:S(2)}) collective-permute-start(bf16[64,1664]{1,0:T(8,128)(2,1)S(1)} %pad_maximum_fusion.8), channel_id=1, source_target_pairs={{0,12},{1,13},{2,14},{3,15},{4,0},{5,1},{6,2},{7,3},{8,4},{9,5},{1... | collective-permute-start | bytes 638984 | tf_op jit(solution)/shard_map/ppermute | solution.py:775
  16.5 1.0 collective-permute-start.2
  17.5 4.2 %collective-permute-start.3 = (bf16[256,1024]{1,0:T(8,128)(2,1)S(1)}, bf16[256,1024]{1,0:T(8,128)(2,1)}, u32[]{:S(2)}, u32[]{:S(2)}) collective-permute-start(bf16[256,1024]{1,0:T(8,128)(2,1)S(1)} %bitcast.193), channel_id=1, source_target_pairs={{0,16},{1,17},{2,18},{3,19},{4,20},{5,21},{6,22},{7,23},{8,24},{9,... | collective-permute-start | bytes 1572872 | tf_op jit(solution)/shard_map/ppermute | solution.py:809
  21.8 1.3 collective-permute-start.4
  23.0 3.6 all-to-all-start
  26.7 7.9 %collective-permute-done.1 = bf16[64,1664]{1,0:T(8,128)(2,1)S(1)} collective-permute-done((bf16[64,1664]{1,0:T(8,128)(2,1)S(1)}, bf16[64,1664]{1,0:T(8,128)(2,1)S(1)}, u32[]{:S(2)}, u32[]{:S(2)}) %collective-permute-start.1) | collective-permute-done | bytes 213024 | tf_op jit(solution)/shard_map/ppermute | solution.py:775
  34.8 1.0 constant_dynamic-slice_fusion.1.packed
  35.8 10.9 %all-to-all-done = bf16[4,2,96,1024]{3,2,1,0:T(8,128)(2,1)S(1)} async-done(((bf16[4,2,96,1024]{3,2,1,0:T(8,128)(2,1)}), bf16[4,2,96,1024]{3,2,1,0:T(8,128)(2,1)S(1)}, u32[]{:S(2)}, u32[]{:S(2)}) %all-to-all-start) | async-done | bytes 1572896 | tf_op jit(solution)/shard_map/all_to_all | solution.py:806
  46.6 1.1 copy-done.14
  48.1 34.7 %weights_gather.1 = (bf16[4,4,64,2048]{3,2,1,0:T(8,128)(2,1)}, bf16[4,4,64,1024]{3,2,1,0:T(8,128)(2,1)}, bf16[4,4,64,256]{3,2,1,0:T(8,128)(2,1)}) custom-call(bf16[4,64,1664]{2,1,0:T(8,128)(2,1)} %constant_dynamic-slice_fusion.1.packed), custom_call_target="tpu_custom_call" | custom-call | flops 1000000 | bytes 16777216 | tf_op jit(solution)/shard_map/weights_gather/pallas_call | solution.py:378
  82.8 2.0 slice_convert_fusion.2
  85.0 1.2 convert_element_type.164
  86.4 1.2 multiply_convert_fusion
  87.6 1.1 copy-done.34
  88.7 2.5 fusion.18
  91.3 0.9 slice.255
  92.7 2.0 copy.87
  94.8 1.2 copy.115
  96.5 2.7 fusion.14
  99.4 1.0 fusion.44
  101.5 5.3 %fusion.87 = (f32[8,2,256]{2,1,0:T(2,128)S(1)}, f32[8,2,256,512]{2,3,1,0:T(8,128)}) fusion(pred[256,512]{0,1:T(8,128)(4,1)S(1)} %fusion.54, bf16[512,8,64,1]{0,2,3,1:T(8,128)(2,1)S(1)} %fusion.51, bf16[256,8,2,64]{0,3,2,1:T(8,128)(2,1)S(1)} %copy-done.22), kind=kOutput, calls=%fused_computation.198 | convolution fusion | flops 276824576 | bytes 9584640 | tf_op jit(solution)/shard_map/sub | solution.py:863
  106.8 4.4 %fusion.24 = bf16[8,64,2,256]{3,1,2,0:T(8,128)(2,1)S(1)} fusion(bf16[512,8,64,1]{0,2,3,1:T(8,128)(2,1)S(1)} %bitcast.214, f32[8,2,256,512]{2,3,1,0:T(8,128)} %get-tuple-element.132, f32[8,2,256]{2,1,0:T(2,128)S(1)} %get-tuple-element.131), kind=kOutput, calls=%fused_computation.46 | convolution fusion | flops 272891904 | bytes 9453568 | tf_op jit(solution)/shard_map/grqk,kgd->qgrd/dot_general | solution.py:866
  111.2 0.8 multiply_reduce_fusion.5
  113.4 43.0 %group_gather.1 = (bf16[8,256,1024]{2,1,0:T(8,128)(2,1)}, f32[8,16,256]{2,1,0:T(8,128)}, bf16[8,256,1024]{2,1,0:T(8,128)(2,1)}) custom-call(bf16[256,1024]{1,0:T(8,128)(2,1)} %copy-done.15, f32[16,256]{1,0:T(8,128)} %fusion.84.refs_1_, bf16[256,1024]{1,0:T(8,128)(2,1)} %bitcast.218), custom_call_target="tpu_custom_call" | custom-call | flops 1000000000 | bytes 16777216 | tf_op jit(solution)/shard_map/group_gather/pallas_call | solution.py:137
  156.3 1.4 constant_dynamic-slice_fusion.gate_ref
  157.8 4.1 all-gather.2.cloned.1.call-done.weights_ref
  161.9 56.2 %expert_layer.1 = (bf16[8,256,1024]{2,1,0:T(8,128)(2,1)}, bf16[8,256,1024]{2,1,0:T(8,128)(2,1)}, f32[8,8,256]{2,1,0:T(8,128)}, bf16[16,2,96,1024]{3,2,1,0:T(8,128)(2,1)}) custom-call(bf16[8,256,1024]{2,1,0:T(8,128)(2,1)} %get-tuple-element.44.rows_ref, bf16[8,256,1024]{2,1,0:T(8,128)(2,1)} %get-tuple-element.45.grad_ref, ...), custom_call_target="tpu_custom_call" | custom-call | flops 44999999488 | bytes 16777216 | tf_op jit(solution)/shard_map/expert_layer/pallas_call | solution.py:699
  218.9 2.2 copy-done.2
  221.1 27.8 %group_reduce.1 = (f32[256,1024]{1,0:T(8,128)S(1)}, f32[8,8,256]{2,1,0:T(8,128)S(1)}) custom-call(bf16[8,256,1024]{2,1,0:T(8,128)(2,1)S(1)} %copy-done.2, f32[8,8,256]{2,1,0:T(8,128)S(1)} %copy-done.4), custom_call_target="tpu_custom_call" | custom-call | flops 1000000 | bytes 16777216 | tf_op jit(solution)/shard_map/group_reduce/pallas_call | solution.py:267
  248.9 2.5 multiply_reduce_fusion.2
  251.5 1.5 subtract_add_fusion
  253.1 1.0 copy-done.7
  254.0 0.8 convolution_convert_fusion.3
  255.1 4.8 %fusion.1 = (f32[8,2,256]{2,1,0:T(2,128)S(1)}, f32[8,512,256,2]{2,1,3,0:T(8,128)S(1)}) fusion(f32[8,2,256,512]{2,3,1,0:T(8,128)} %get-tuple-element.132, f32[8,2,256]{2,1,0:T(2,128)S(1)} %get-tuple-element.131, bf16[512,8,64,1]{0,2,3,1:T(8,128)(2,1)S(1)} %bitcast.215, bf16[256,8,2,64]{0,3,2,1:T(8,128)(2,1)S(1)} %bitcast.216), kind=kOutput, calls=%fused_computation.3 | convolution fusion | flops 274722816 | bytes 17858560 | tf_op jit(solution)/shard_map/qgrd,kgd->grqk/dot_general | solution.py:901
  259.9 0.9 slice-done.1
  260.9 1.5 fusion.3
  262.4 0.8 fusion.28
  263.7 0.8 copy-done.23
  264.4 1.4 fusion.20
  265.8 1.4 fusion.8
  267.3 1.8 collective-permute-start.5
  269.1 1.8 convolution_convert_fusion.2
  271.0 0.8 fusion.12
  272.5 2.0 convolution_convert_fusion
  274.5 8.2 %collective-permute-done.5 = bf16[256,1024]{0,1:T(8,128)(2,1)S(1)} collective-permute-done((bf16[256,1024]{0,1:T(8,128)(2,1)S(1)}, bf16[256,1024]{0,1:T(8,128)(2,1)S(1)}, u32[]{:S(2)}, u32[]{:S(2)}) %collective-permute-start.5) | collective-permute-done | bytes 524320 | tf_op jit(solution)/shard_map/ppermute | solution.py:914
  283.2 1.9 fusion.36
  285.2 1.1 select_maximum_fusion
  286.3 1.6 copy.97
  287.8 3.2 convolution_convert_fusion.1
  291.0 57.7 %weights_reduce.1 = (bf16[4,64,1664]{2,1,0:T(8,128)(2,1)S(1)}, bf16[4,64,1024]{2,1,0:T(8,128)(2,1)S(1)}) custom-call(bf16[4,4,64,1024]{3,2,1,0:T(8,128)(2,1)S(1)} %bitcast.185, bf16[4,4,64,1024]{3,2,1,0:T(8,128)(2,1)} %bitcast.197, bf16[4,4,64,1024]{3,2,1,0:T(8,128)(2,1)} %bitcast.196, f32[4,4,64,256]{3,2,1,0:T(8,128)S(1)} %bitcast.186, ...), custom_call_target="tpu_custom_call" | custom-call | flops 1000000 | bytes 16777216 | tf_op jit(solution)/shard_map/weights_reduce/pallas_call | solution.py:521
  348.8 0.9 multiply_reduce_fusion.1
  349.6 1.6 pad_maximum_fusion.12
  351.2 0.9 fusion.47
  352.2 1.1 fusion.52
  353.3 1.5 collective-permute-done.6
  354.8 1.9 sqrt_bitcast_fusion
  356.7 44.0 %send_pieces.1 = (bf16[8,2,96,1024]{3,2,1,0:T(8,128)(2,1)}, bf16[2,64,1664]{2,1,0:T(8,128)(2,1)}) custom-call(bf16[4,2,96,1024]{3,2,1,0:T(8,128)(2,1)} %reduce-scatter.2.cloned.1.call-done.pieces, bf16[4,64,1664]{2,1,0:T(8,128)(2,1)} %copy-done.3), custom_call_target="tpu_custom_call" | custom-call | tf_op jit(solution)/shard_map/send_pieces/pallas_call | solution.py:601
  400.7 1.8 slice.188
  402.5 1.4 slice.189
  404.6 3.2 convert_bitcast_fusion
  407.8 1.9 convert_bitcast_fusion.1
  411.2 0.8 maximum_convert_fusion
  (156 shorter events, 10.2 us)
Async XLA Ops:
  7.2 1.5 copy-start
  8.9 2.1 copy-start.36
  8.9 2.1 copy-start.37
  8.9 2.2 copy-start.32
  8.9 2.3 copy-start.29
  9.0 2.3 copy-start.30
  9.0 8.5 %copy-start.10 = (bf16[1,256,1024]{2,1,0:T(8,128)(2,1)S(1)}, bf16[1,256,1024]{2,1,0:T(8,128)(2,1)}, u32[]{:S(2)}) copy-start(bf16[1,256,1024]{2,1,0:T(8,128)(2,1)} %param.11) | copy-start | bytes 1572868
  9.0 12.8 %copy-start.33 = (s32[1,256]{1,0:T(1,128)S(1)}, s32[1,256]{1,0:T(1,128)}, u32[]{:S(2)}) copy-start(s32[1,256]{1,0:T(1,128)} %param.12) | copy-start | bytes 3076
  11.4 15.3 %collective-permute-start = (bf16[64,1664]{1,0:T(8,128)(2,1)S(1)}, bf16[64,1664]{1,0:T(8,128)(2,1)S(1)}, u32[]{:S(2)}, u32[]{:S(2)}) collective-permute-start(bf16[64,1664]{1,0:T(8,128)(2,1)S(1)} %pad_maximum_fusion.8), channel_id=1, source_target_pairs={{0,12},{1,13},{2,14},{3,15},{4,0},{5,1},{6,2},{7,3},{8,4},{9,5},{1... | collective-permute-start | bytes 638984 | tf_op jit(solution)/shard_map/ppermute | solution.py:775
  16.5 18.1 %collective-permute-start.1 = (bf16[64,1664]{1,0:T(8,128)(2,1)S(1)}, bf16[64,1664]{1,0:T(8,128)(2,1)S(1)}, u32[]{:S(2)}, u32[]{:S(2)}) collective-permute-start(bf16[64,1664]{1,0:T(8,128)(2,1)S(1)} %pad_maximum_fusion.8), channel_id=1, source_target_pairs={{0,8},{1,9},{2,10},{3,11},{4,12},{5,13},{6,14},{7,15},{8,0},{9,1},... | collective-permute-start | bytes 638984 | tf_op jit(solution)/shard_map/ppermute | solution.py:775
  16.5 18.1 %collective-permute-start.2 = (bf16[64,1664]{1,0:T(8,128)(2,1)S(1)}, bf16[64,1664]{1,0:T(8,128)(2,1)S(1)}, u32[]{:S(2)}, u32[]{:S(2)}) collective-permute-start(bf16[64,1664]{1,0:T(8,128)(2,1)S(1)} %pad_maximum_fusion.8), channel_id=1, source_target_pairs={{0,4},{1,5},{2,6},{3,7},{4,8},{5,9},{6,10},{7,11},{8,12},{9,13},{1... | collective-permute-start | bytes 638984 | tf_op jit(solution)/shard_map/ppermute | solution.py:775
  17.5 18.2 %collective-permute-start.3 = (bf16[256,1024]{1,0:T(8,128)(2,1)S(1)}, bf16[256,1024]{1,0:T(8,128)(2,1)}, u32[]{:S(2)}, u32[]{:S(2)}) collective-permute-start(bf16[256,1024]{1,0:T(8,128)(2,1)S(1)} %bitcast.193), channel_id=1, source_target_pairs={{0,16},{1,17},{2,18},{3,19},{4,20},{5,21},{6,22},{7,23},{8,24},{9,... | collective-permute-start | bytes 1572872 | tf_op jit(solution)/shard_map/ppermute | solution.py:809
  21.8 14.0 %collective-permute-start.4 = (s32[1,256]{1,0:T(1,128)S(1)}, s32[1,256]{1,0:T(1,128)S(1)}, u32[]{:S(2)}, u32[]{:S(2)}) collective-permute-start(s32[1,256]{1,0:T(1,128)S(1)} %copy-done.33), channel_id=1, source_target_pairs={{0,16},{1,17},{2,18},{3,19},{4,20},{5,21},{6,22},{7,23},{8,24},{9,... | collective-permute-start | bytes 3080 | tf_op jit(solution)/shard_map/ppermute | solution.py:810
  23.0 23.6 %all-to-all-start = ((bf16[4,2,96,1024]{3,2,1,0:T(8,128)(2,1)}), bf16[4,2,96,1024]{3,2,1,0:T(8,128)(2,1)S(1)}, u32[]{:S(2)}, u32[]{:S(2)}) async-start(bf16[4,2,96,1024]{3,2,1,0:T(8,128)(2,1)} %bitcast.198), calls=%async_computation | async-start | bytes 3145728 | tf_op jit(solution)/shard_map/all_to_all | solution.py:806
  26.6 135.2 %all-gather.2.cloned.1.call-start = ((), (), s32[]{:S(2)}) async-start(), calls=%async_computation.2 | async-start | bytes 7864320 | tf_op jit(solution)/shard_map/all_gather | solution.py:827
  34.7 13.2 %copy-start.31 = (s32[1,256,8]{1,2,0:T(8,128)S(1)}, s32[1,256,8]{1,2,0:T(8,128)}, u32[]{:S(2)}) copy-start(s32[1,256,8]{1,2,0:T(8,128)} %param.13) | copy-start | bytes 24580
  46.6 1.1 copy-start.14
  47.8 308.9 %reduce-scatter.2.cloned.1.call-start = ((), (), s32[]{:S(2)}) async-start(), calls=%async_computation.3 | async-start | bytes 7864320 | tf_op jit(solution)/shard_map/reduce_scatter | solution.py:881
  86.1 2.6 copy-start.34
  100.4 1.0 copy-start.22
  101.5 5.3 %copy-start.17 = (bf16[512,8,64,1]{0,2,3,1:T(8,128)(2,1)}, bf16[512,8,64,1]{0,2,3,1:T(8,128)(2,1)S(1)}, u32[]{:S(2)}) copy-start(bf16[512,8,64,1]{0,2,3,1:T(8,128)(2,1)S(1)} %fusion.51) | copy-start | bytes 1572868
  101.5 5.3 %copy-start.26 = (bf16[512,512]{0,1:T(8,128)(2,1)S(1)}, bf16[512,512]{0,1:T(8,128)(2,1)}, u32[]{:S(2)}) copy-start(bf16[512,512]{0,1:T(8,128)(2,1)} %copy.87) | copy-start | bytes 1572868
  106.8 4.4 %copy-start.12 = (bf16[4,4,64,1024]{3,2,1,0:T(8,128)(2,1)S(1)}, bf16[4,4,64,1024]{3,2,1,0:T(8,128)(2,1)}, u32[]{:S(2)}) copy-start(bf16[4,4,64,1024]{3,2,1,0:T(8,128)(2,1)} %get-tuple-element.43) | copy-start | bytes 6291460
  111.2 0.9 copy-start.19
  111.2 1.2 copy-start.21
  112.0 139.5 %copy-start.5 = (f32[256,1024]{1,0:T(8,128)}, f32[256,1024]{1,0:T(8,128)S(1)}, u32[]{:S(2)}) copy-start(f32[256,1024]{1,0:T(8,128)S(1)} %get-tuple-element.134) | copy-start | bytes 3145732
  112.4 0.9 copy-start.15
  218.1 0.8 copy-start.4
  218.9 2.2 copy-start.2
  251.5 2.5 copy-start.13
  253.0 1.0 copy-start.7
  254.0 1.0 copy-start.27
  255.0 4.9 %slice-start = ((s8[8388608]{0:T(1024)(128)(4,1)}), s8[4194304]{0:T(1024)(128)(4,1)S(1)}, s32[]{:S(2)}) async-start(s8[8388608]{0:T(1024)(128)(4,1)} %bitcast.191), calls=%async_computation.4 | async-start | bytes 8388608
  255.1 5.8 %slice-start.1 = ((s8[8388608]{0:T(1024)(128)(4,1)}), s8[4194304]{0:T(1024)(128)(4,1)S(1)}, s32[]{:S(2)}) async-start(s8[8388608]{0:T(1024)(128)(4,1)} %bitcast.191), calls=%async_computation.5 | async-start | bytes 8388608
  260.9 1.5 copy-start.18
  263.4 1.0 copy-start.23
  267.2 3.7 copy-start.35
  267.3 15.4 %collective-permute-start.5 = (bf16[256,1024]{0,1:T(8,128)(2,1)S(1)}, bf16[256,1024]{0,1:T(8,128)(2,1)S(1)}, u32[]{:S(2)}, u32[]{:S(2)}) collective-permute-start(bf16[256,1024]{0,1:T(8,128)(2,1)S(1)} %fusion.40), channel_id=1, source_target_pairs={{16,0},{17,1},{18,2},{19,3},{20,4},{21,5},{22,6},{23,7},{24,8},{25... | collective-permute-start | bytes 1572872 | tf_op jit(solution)/shard_map/ppermute | solution.py:914
  270.9 1.0 copy-start.16
  270.9 1.4 copy-start.8
  271.0 1.5 copy-start.20
  283.2 2.0 copy-start.24
  291.0 60.2 %copy-start.6 = (f32[256,1024]{1,0:T(8,128)S(1)}, f32[256,1024]{1,0:T(8,128)}, u32[]{:S(2)}) copy-start(f32[256,1024]{1,0:T(8,128)} %copy-done.5) | copy-start | bytes 3145732
  348.7 4.6 %copy-start.3 = (bf16[4,64,1664]{2,1,0:T(8,128)(2,1)}, bf16[4,64,1664]{2,1,0:T(8,128)(2,1)S(1)}, u32[]{:S(2)}) copy-start(bf16[4,64,1664]{2,1,0:T(8,128)(2,1)S(1)} %get-tuple-element.55.packed) | copy-start | bytes 2555908
  348.7 3.4 copy-start.9
  348.8 3.4 copy-start.11
  348.8 3.4 copy-start.25
  351.2 3.6 collective-permute-start.6
  402.5 1.4 copy-start.28
  404.6 7.4 %copy-start.1 = (bf16[32,16,1024]{2,1,0:T(8,128)(2,1)S(1)}, bf16[32,16,1024]{2,1,0:T(8,128)(2,1)}, u32[]{:S(2)}) copy-start(bf16[32,16,1024]{2,1,0:T(8,128)(2,1)} %param.20) | copy-start | bytes 3145732
Sparse Core Ops, SparseCore 0:
  47.9 113.8 all-gather.1
  218.2 108.9 reduce-scatter.1

commit v4 on v2

--- a/solution.py
+++ b/solution.py
@@ -544,7 +544,7 @@
     home = lax.axis_index("dp") // PLACES
     keep = pltpu.make_async_copy(pieces.at[place], whole.at[rank], local)
     keep.start()
-    masks = (6, 7, 2, 4, 3, 5, 1)
+    masks = (4, 2, 6, 5, 3, 7, 1)
     others = [(home + k) % groups for k in range(1, groups)]
     far = [{"seq": seq, "dp": g * PLACES + place} for g in others]
     meet([peer(mask) for mask in masks] + far)

time: 425 us -> 425 us (level)
  no operation moved by 1% of the time
where the time goes in v4:
time: 425 us; the launch traced here: 423 us
  Pallas kernels  264 us (62%)
  waiting for transfers between devices  38.3 us (9%)
  matrix products  34.5 us (8%)
  local copies, waits for them, and re-layouts  29.4 us (7%)
  other arithmetic  25.3 us (6%)
  starting transfers between devices  16.8 us (4%)
  between operations  15 us (4%)
    pallas_call x1, Pallas kernels, weights_reduce(): pl.pallas_call(functools.partial(weights_reduce_kernel, count), out_shape...  58 us
    pallas_call x1, Pallas kernels, expert_layer(): pl.pallas_call(functools.partial(expert_kernel, first), grid=(GROUP // sh...  56.2 us
    pallas_call x1, Pallas kernels, send_pieces(): pl.pallas_call(pieces_kernel, out_shape=[jax.ShapeDtypeStruct((GROUP,) +...  44.6 us
    pallas_call x1, Pallas kernels, group_gather(): pl.pallas_call(functools.partial(gather_kernel, count), out_shape=[jax.Sh...  42.9 us
    pallas_call x1, Pallas kernels, weights_gather(): pl.pallas_call(functools.partial(weights_gather_kernel, halves), out_shap...  34.7 us
    pallas_call x1, Pallas kernels, group_reduce(): pl.pallas_call(reduce_kernel, out_shape=[jax.ShapeDtypeStruct((rows, widt...  27.8 us
    unnamed x93, local copies, waits for them, and re-layouts  14.4 us
    ppermute x1, waiting for transfers between devices, body(): kv_back = lax.ppermute(kv_grad[:count].astype(bf16), 'seq', back_pair)  12.8 us
  transfers between devices with their start and end apart: 10, of which 5 were waited for; matrix products, arithmetic and copies ran while one was open for 15% of the time, Pallas kernels for 39%

profile of v4, /device:TPU:0, one launch (start us, length us, event | category | flops | bytes accessed | tf_op | source)
XLA Modules:
  0.0 423.5 jit_solution(1410636639820898692)
XLA Ops:
  7.2 1.4 dynamic-slice_bitcast_fusion
  9.0 2.0 copy.83
  11.4 5.1 %collective-permute-start = (bf16[64,1664]{1,0:T(8,128)(2,1)S(1)}, bf16[64,1664]{1,0:T(8,128)(2,1)S(1)}, u32[]{:S(2)}, u32[]{:S(2)}) collective-permute-start(bf16[64,1664]{1,0:T(8,128)(2,1)S(1)} %pad_maximum_fusion.8), channel_id=1, source_target_pairs={{0,12},{1,13},{2,14},{3,15},{4,0},{5,1},{6,2},{7,3},{8,4},{9,5},{1... | collective-permute-start | bytes 638984 | tf_op jit(solution)/shard_map/ppermute | solution.py:775
  16.5 1.0 collective-permute-start.2
  17.5 4.2 %collective-permute-start.3 = (bf16[256,1024]{1,0:T(8,128)(2,1)S(1)}, bf16[256,1024]{1,0:T(8,128)(2,1)}, u32[]{:S(2)}, u32[]{:S(2)}) collective-permute-start(bf16[256,1024]{1,0:T(8,128)(2,1)S(1)} %bitcast.187), channel_id=1, source_target_pairs={{0,16},{1,17},{2,18},{3,19},{4,20},{5,21},{6,22},{7,23},{8,24},{9,... | collective-permute-start | bytes 1572872 | tf_op jit(solution)/shard_map/ppermute | solution.py:809
  21.8 1.3 collective-permute-start.4
  23.0 3.6 all-to-all-start
  26.7 7.8 %collective-permute-done.1 = bf16[64,1664]{1,0:T(8,128)(2,1)S(1)} collective-permute-done((bf16[64,1664]{1,0:T(8,128)(2,1)S(1)}, bf16[64,1664]{1,0:T(8,128)(2,1)S(1)}, u32[]{:S(2)}, u32[]{:S(2)}) %collective-permute-start.1) | collective-permute-done | bytes 213024 | tf_op jit(solution)/shard_map/ppermute | solution.py:775
  34.8 1.0 constant_dynamic-slice_fusion.1.packed
  35.8 10.9 %all-to-all-done = bf16[4,2,96,1024]{3,2,1,0:T(8,128)(2,1)S(1)} async-done(((bf16[4,2,96,1024]{3,2,1,0:T(8,128)(2,1)}), bf16[4,2,96,1024]{3,2,1,0:T(8,128)(2,1)S(1)}, u32[]{:S(2)}, u32[]{:S(2)}) %all-to-all-start) | async-done | bytes 1572896 | tf_op jit(solution)/shard_map/all_to_all | solution.py:806
  46.6 1.1 copy-done.14
  48.1 34.7 %weights_gather.1 = (bf16[4,4,64,2048]{3,2,1,0:T(8,128)(2,1)}, bf16[4,4,64,1024]{3,2,1,0:T(8,128)(2,1)}, bf16[4,4,64,256]{3,2,1,0:T(8,128)(2,1)}) custom-call(bf16[4,64,1664]{2,1,0:T(8,128)(2,1)} %constant_dynamic-slice_fusion.1.packed), custom_call_target="tpu_custom_call" | custom-call | flops 1000000 | bytes 16777216 | tf_op jit(solution)/shard_map/weights_gather/pallas_call | solution.py:378
  82.8 2.0 slice_convert_fusion.2
  85.0 1.2 convert_element_type.159
  86.6 1.0 copy-done.24
  87.6 1.1 copy-done.36
  88.7 1.3 fusion.10
  90.1 0.9 slice.235
  91.5 2.0 copy.87
  93.6 1.2 copy.115
  95.3 2.7 fusion.8
  98.2 1.0 fusion.37
  99.5 0.7 copy-done.22
  100.3 5.3 %fusion.80 = (f32[8,2,256]{2,1,0:T(2,128)S(1)}, f32[8,2,256,512]{2,3,1,0:T(8,128)}) fusion(pred[256,512]{0,1:T(8,128)(4,1)S(1)} %fusion.47, bf16[512,8,64,1]{0,2,3,1:T(8,128)(2,1)S(1)} %fusion.44, bf16[256,8,2,64]{0,3,2,1:T(8,128)(2,1)S(1)} %copy-done.22), kind=kOutput, calls=%fused_computation.190 | convolution fusion | flops 276824576 | bytes 9584640 | tf_op jit(solution)/shard_map/sub | solution.py:863
  105.6 4.4 %fusion.17 = bf16[8,64,2,256]{3,1,2,0:T(8,128)(2,1)S(1)} fusion(bf16[512,8,64,1]{0,2,3,1:T(8,128)(2,1)S(1)} %bitcast.207, f32[8,2,256,512]{2,3,1,0:T(8,128)} %get-tuple-element.130, f32[8,2,256]{2,1,0:T(2,128)S(1)} %get-tuple-element.129), kind=kOutput, calls=%fused_computation.40 | convolution fusion | flops 272891904 | bytes 9453568 | tf_op jit(solution)/shard_map/grqk,kgd->qgrd/dot_general | solution.py:866
  110.0 0.8 multiply_reduce_fusion.5
  112.2 42.9 %group_gather.1 = (bf16[8,256,1024]{2,1,0:T(8,128)(2,1)}, f32[8,16,256]{2,1,0:T(8,128)}, bf16[8,256,1024]{2,1,0:T(8,128)(2,1)}) custom-call(bf16[256,1024]{1,0:T(8,128)(2,1)} %copy-done.15, f32[16,256]{1,0:T(8,128)} %fusion.77.refs_1_, bf16[256,1024]{1,0:T(8,128)(2,1)} %bitcast.211), custom_call_target="tpu_custom_call" | custom-call | flops 1000000000 | bytes 16777216 | tf_op jit(solution)/shard_map/group_gather/pallas_call | solution.py:137
  155.1 1.5 constant_dynamic-slice_fusion.gate_ref
  156.6 5.3 %all-gather.2.cloned.1.call-done.weights_ref = bf16[16,2,96,1024]{3,2,1,0:T(8,128)(2,1)} async-done(((bf16[4,2,96,1024]{3,2,1,0:T(8,128)(2,1)}), bf16[16,2,96,1024]{3,2,1,0:T(8,128)(2,1)}) %all-gather.2.cloned.1.call-update) | async-done | bytes 6291472 | tf_op jit(solution)/shard_map/all_gather | solution.py:827
  161.9 56.2 %expert_layer.1 = (bf16[8,256,1024]{2,1,0:T(8,128)(2,1)}, bf16[8,256,1024]{2,1,0:T(8,128)(2,1)}, f32[8,8,256]{2,1,0:T(8,128)}, bf16[16,2,96,1024]{3,2,1,0:T(8,128)(2,1)}) custom-call(bf16[8,256,1024]{2,1,0:T(8,128)(2,1)} %get-tuple-element.44.rows_ref, bf16[8,256,1024]{2,1,0:T(8,128)(2,1)} %get-tuple-element.45.grad_ref, ...), custom_call_target="tpu_custom_call" | custom-call | flops 44999999488 | bytes 16777216 | tf_op jit(solution)/shard_map/expert_layer/pallas_call | solution.py:699
  218.9 2.2 copy-done.2
  221.1 27.8 %group_reduce.1 = (f32[256,1024]{1,0:T(8,128)S(1)}, f32[8,8,256]{2,1,0:T(8,128)S(1)}) custom-call(bf16[8,256,1024]{2,1,0:T(8,128)(2,1)S(1)} %copy-done.2, f32[8,8,256]{2,1,0:T(8,128)S(1)} %copy-done.4), custom_call_target="tpu_custom_call" | custom-call | flops 1000000 | bytes 16777216 | tf_op jit(solution)/shard_map/group_reduce/pallas_call | solution.py:267
  248.9 2.5 multiply_reduce_fusion.2
  251.5 1.5 subtract_add_fusion
  253.0 1.0 copy-done.7
  254.0 0.8 convolution_convert_fusion.2
  255.0 4.8 %fusion.1 = (f32[8,2,256]{2,1,0:T(2,128)S(1)}, f32[8,512,256,2]{2,1,3,0:T(8,128)S(1)}) fusion(f32[8,2,256,512]{2,3,1,0:T(8,128)} %get-tuple-element.130, f32[8,2,256]{2,1,0:T(2,128)S(1)} %get-tuple-element.129, bf16[512,8,64,1]{0,2,3,1:T(8,128)(2,1)S(1)} %bitcast.208, bf16[256,8,2,64]{0,3,2,1:T(8,128)(2,1)S(1)} %bitcast.209), kind=kOutput, calls=%fused_computation.3 | convolution fusion | flops 274722816 | bytes 17858560 | tf_op jit(solution)/shard_map/qgrd,kgd->grqk/dot_general | solution.py:901
  259.9 0.9 slice-done.1
  260.8 1.5 fusion.3
  262.4 0.8 fusion.21
  263.6 0.8 copy-done.23
  264.4 1.4 fusion.16
  265.8 1.4 fusion.12
  267.3 1.4 collective-permute-start.5
  269.8 12.8 %collective-permute-done.5 = bf16[256,1024]{0,1:T(8,128)(2,1)S(1)} collective-permute-done((bf16[256,1024]{0,1:T(8,128)(2,1)S(1)}, bf16[256,1024]{0,1:T(8,128)(2,1)S(1)}, u32[]{:S(2)}, u32[]{:S(2)}) %collective-permute-start.5) | collective-permute-done | bytes 524320 | tf_op jit(solution)/shard_map/ppermute | solution.py:914
  283.1 2.0 copy-done.37
  285.1 2.4 fusion.29
  287.6 1.1 select_maximum_fusion
  288.6 1.6 copy.97
  290.2 4.6 %convolution_convert_fusion = bf16[1024,2048]{1,0:T(8,128)(2,1)} fusion(bf16[512,1024]{1,0:T(8,128)(2,1)} %copy-done.24, bf16[256,512]{0,1:T(8,128)(2,1)S(1)} %get-tuple-element.114, bf16[256,512]{0,1:T(8,128)(2,1)} %copy-done.30, bf16[256,1024]{0,1:T(8,128)(2,1)} %copy-done.28), kind=kOutput, calls=%fused_computation.14 | convolution fusion | flops 1078984704 | bytes 5767168 | tf_op jit(solution)/shard_map/dot_general | solution.py:922
  294.8 58.0 %weights_reduce.1 = (bf16[4,64,1664]{2,1,0:T(8,128)(2,1)S(1)}, bf16[4,64,1024]{2,1,0:T(8,128)(2,1)S(1)}) custom-call(bf16[4,4,64,2048]{3,2,1,0:T(8,128)(2,1)} %bitcast.196, bf16[4,4,64,1024]{3,2,1,0:T(8,128)(2,1)S(1)} %bitcast.179, f32[4,4,64,256]{3,2,1,0:T(8,128)S(1)} %bitcast.180, bf16[8,4,64,1024]{3,2,1,0:T(8,128)(2,1)} %bitcast.195), custom_call_target="tpu_custom_call" | custom-call | flops 1000000 | bytes 16777216 | tf_op jit(solution)/shard_map/weights_reduce/pallas_call | solution.py:521
  352.8 0.9 multiply_reduce_fusion.1
  353.7 1.6 pad_maximum_fusion.12
  355.3 0.9 fusion.40
  356.3 1.1 fusion.45
  357.4 1.5 collective-permute-done.6
  358.8 1.9 sqrt_bitcast_fusion
  360.7 44.6 %send_pieces.1 = (bf16[8,2,96,1024]{3,2,1,0:T(8,128)(2,1)}, bf16[2,64,1664]{2,1,0:T(8,128)(2,1)}) custom-call(bf16[4,2,96,1024]{3,2,1,0:T(8,128)(2,1)} %reduce-scatter.2.cloned.1.call-done.pieces, bf16[4,64,1664]{2,1,0:T(8,128)(2,1)} %copy-done.3), custom_call_target="tpu_custom_call" | custom-call | tf_op jit(solution)/shard_map/send_pieces/pallas_call | solution.py:601
  405.3 1.8 slice.178
  407.1 1.4 slice.179
  409.3 3.2 convert_bitcast_fusion
  412.5 1.9 convert_bitcast_fusion.1
  415.1 0.7 maximum_convert_fusion.1
  415.8 0.8 maximum_convert_fusion
  (159 shorter events, 9.3 us)
Async XLA Ops:
  7.2 1.5 copy-start
  8.9 2.1 copy-start.38
  8.9 2.1 copy-start.39
  8.9 2.2 copy-start.34
  8.9 2.3 copy-start.31
  9.0 2.3 copy-start.32
  9.0 8.5 %copy-start.10 = (bf16[1,256,1024]{2,1,0:T(8,128)(2,1)S(1)}, bf16[1,256,1024]{2,1,0:T(8,128)(2,1)}, u32[]{:S(2)}) copy-start(bf16[1,256,1024]{2,1,0:T(8,128)(2,1)} %param.11) | copy-start | bytes 1572868
  9.0 12.8 %copy-start.35 = (s32[1,256]{1,0:T(1,128)S(1)}, s32[1,256]{1,0:T(1,128)}, u32[]{:S(2)}) copy-start(s32[1,256]{1,0:T(1,128)} %param.12) | copy-start | bytes 3076
  11.4 15.3 %collective-permute-start = (bf16[64,1664]{1,0:T(8,128)(2,1)S(1)}, bf16[64,1664]{1,0:T(8,128)(2,1)S(1)}, u32[]{:S(2)}, u32[]{:S(2)}) collective-permute-start(bf16[64,1664]{1,0:T(8,128)(2,1)S(1)} %pad_maximum_fusion.8), channel_id=1, source_target_pairs={{0,12},{1,13},{2,14},{3,15},{4,0},{5,1},{6,2},{7,3},{8,4},{9,5},{1... | collective-permute-start | bytes 638984 | tf_op jit(solution)/shard_map/ppermute | solution.py:775
  16.5 18.1 %collective-permute-start.1 = (bf16[64,1664]{1,0:T(8,128)(2,1)S(1)}, bf16[64,1664]{1,0:T(8,128)(2,1)S(1)}, u32[]{:S(2)}, u32[]{:S(2)}) collective-permute-start(bf16[64,1664]{1,0:T(8,128)(2,1)S(1)} %pad_maximum_fusion.8), channel_id=1, source_target_pairs={{0,8},{1,9},{2,10},{3,11},{4,12},{5,13},{6,14},{7,15},{8,0},{9,1},... | collective-permute-start | bytes 638984 | tf_op jit(solution)/shard_map/ppermute | solution.py:775
  16.5 18.1 %collective-permute-start.2 = (bf16[64,1664]{1,0:T(8,128)(2,1)S(1)}, bf16[64,1664]{1,0:T(8,128)(2,1)S(1)}, u32[]{:S(2)}, u32[]{:S(2)}) collective-permute-start(bf16[64,1664]{1,0:T(8,128)(2,1)S(1)} %pad_maximum_fusion.8), channel_id=1, source_target_pairs={{0,4},{1,5},{2,6},{3,7},{4,8},{5,9},{6,10},{7,11},{8,12},{9,13},{1... | collective-permute-start | bytes 638984 | tf_op jit(solution)/shard_map/ppermute | solution.py:775
  17.5 18.2 %collective-permute-start.3 = (bf16[256,1024]{1,0:T(8,128)(2,1)S(1)}, bf16[256,1024]{1,0:T(8,128)(2,1)}, u32[]{:S(2)}, u32[]{:S(2)}) collective-permute-start(bf16[256,1024]{1,0:T(8,128)(2,1)S(1)} %bitcast.187), channel_id=1, source_target_pairs={{0,16},{1,17},{2,18},{3,19},{4,20},{5,21},{6,22},{7,23},{8,24},{9,... | collective-permute-start | bytes 1572872 | tf_op jit(solution)/shard_map/ppermute | solution.py:809
  21.8 14.0 %collective-permute-start.4 = (s32[1,256]{1,0:T(1,128)S(1)}, s32[1,256]{1,0:T(1,128)S(1)}, u32[]{:S(2)}, u32[]{:S(2)}) collective-permute-start(s32[1,256]{1,0:T(1,128)S(1)} %copy-done.35), channel_id=1, source_target_pairs={{0,16},{1,17},{2,18},{3,19},{4,20},{5,21},{6,22},{7,23},{8,24},{9,... | collective-permute-start | bytes 3080 | tf_op jit(solution)/shard_map/ppermute | solution.py:810
  23.0 23.6 %all-to-all-start = ((bf16[4,2,96,1024]{3,2,1,0:T(8,128)(2,1)}), bf16[4,2,96,1024]{3,2,1,0:T(8,128)(2,1)S(1)}, u32[]{:S(2)}, u32[]{:S(2)}) async-start(bf16[4,2,96,1024]{3,2,1,0:T(8,128)(2,1)} %bitcast.190), calls=%async_computation | async-start | bytes 3145728 | tf_op jit(solution)/shard_map/all_to_all | solution.py:806
  26.6 135.2 %all-gather.2.cloned.1.call-start = ((), (), s32[]{:S(2)}) async-start(), calls=%async_computation.2 | async-start | bytes 7864320 | tf_op jit(solution)/shard_map/all_gather | solution.py:827
  34.7 13.2 %copy-start.33 = (s32[1,256,8]{1,2,0:T(8,128)S(1)}, s32[1,256,8]{1,2,0:T(8,128)}, u32[]{:S(2)}) copy-start(s32[1,256,8]{1,2,0:T(8,128)} %param.13) | copy-start | bytes 24580
  46.6 1.1 copy-start.14
  47.8 312.9 %reduce-scatter.2.cloned.1.call-start = ((), (), s32[]{:S(2)}) async-start(), calls=%async_computation.3 | async-start | bytes 7864320 | tf_op jit(solution)/shard_map/reduce_scatter | solution.py:881
  86.1 2.6 copy-start.36
  86.6 1.0 copy-start.24
  99.2 1.0 copy-start.22
  100.3 5.3 %copy-start.17 = (bf16[512,8,64,1]{0,2,3,1:T(8,128)(2,1)}, bf16[512,8,64,1]{0,2,3,1:T(8,128)(2,1)S(1)}, u32[]{:S(2)}) copy-start(bf16[512,8,64,1]{0,2,3,1:T(8,128)(2,1)S(1)} %fusion.44) | copy-start | bytes 1572868
  100.3 5.3 %copy-start.26 = (bf16[512,512]{0,1:T(8,128)(2,1)S(1)}, bf16[512,512]{0,1:T(8,128)(2,1)}, u32[]{:S(2)}) copy-start(bf16[512,512]{0,1:T(8,128)(2,1)} %copy.87) | copy-start | bytes 1572868
  105.6 4.5 %copy-start.12 = (bf16[4,4,64,1024]{3,2,1,0:T(8,128)(2,1)S(1)}, bf16[4,4,64,1024]{3,2,1,0:T(8,128)(2,1)}, u32[]{:S(2)}) copy-start(bf16[4,4,64,1024]{3,2,1,0:T(8,128)(2,1)} %get-tuple-element.43) | copy-start | bytes 6291460
  110.0 0.9 copy-start.19
  110.0 1.2 copy-start.21
  110.9 140.6 %copy-start.5 = (f32[256,1024]{1,0:T(8,128)}, f32[256,1024]{1,0:T(8,128)S(1)}, u32[]{:S(2)}) copy-start(f32[256,1024]{1,0:T(8,128)S(1)} %get-tuple-element.132) | copy-start | bytes 3145732
  111.3 0.9 copy-start.15
  218.1 0.8 copy-start.4
  218.9 2.2 copy-start.2
  251.5 2.5 copy-start.13
  253.0 1.0 copy-start.7
  254.0 1.0 copy-start.27
  255.0 4.9 %slice-start = ((s8[8388608]{0:T(1024)(128)(4,1)}), s8[4194304]{0:T(1024)(128)(4,1)S(1)}, s32[]{:S(2)}) async-start(s8[8388608]{0:T(1024)(128)(4,1)} %bitcast.185), calls=%async_computation.4 | async-start | bytes 8388608
  255.0 5.8 %slice-start.1 = ((s8[8388608]{0:T(1024)(128)(4,1)}), s8[4194304]{0:T(1024)(128)(4,1)S(1)}, s32[]{:S(2)}) async-start(s8[8388608]{0:T(1024)(128)(4,1)} %bitcast.185), calls=%async_computation.5 | async-start | bytes 8388608
  260.8 1.5 copy-start.18
  263.3 1.0 copy-start.23
  264.4 18.7 %copy-start.28 = (bf16[256,1024]{0,1:T(8,128)(2,1)}, bf16[256,1024]{0,1:T(8,128)(2,1)S(1)}, u32[]{:S(2)}) copy-start(bf16[256,1024]{0,1:T(8,128)(2,1)S(1)} %fusion.39) | copy-start | bytes 1572868
  267.2 1.5 copy-start.16
  267.2 1.9 copy-start.8
  267.2 1.9 copy-start.20
  267.3 15.3 %collective-permute-start.5 = (bf16[256,1024]{0,1:T(8,128)(2,1)S(1)}, bf16[256,1024]{0,1:T(8,128)(2,1)S(1)}, u32[]{:S(2)}, u32[]{:S(2)}) collective-permute-start(bf16[256,1024]{0,1:T(8,128)(2,1)S(1)} %fusion.33), channel_id=1, source_target_pairs={{16,0},{17,1},{18,2},{19,3},{20,4},{21,5},{22,6},{23,7},{24,8},{25... | collective-permute-start | bytes 1572872 | tf_op jit(solution)/shard_map/ppermute | solution.py:914
  282.8 2.3 copy-start.37
  283.1 4.5 %copy-start.30 = (bf16[256,512]{0,1:T(8,128)(2,1)}, bf16[256,512]{0,1:T(8,128)(2,1)S(1)}, u32[]{:S(2)}) copy-start(bf16[256,512]{0,1:T(8,128)(2,1)S(1)} %fusion.46) | copy-start | bytes 786436
  294.8 60.5 %copy-start.6 = (f32[256,1024]{1,0:T(8,128)S(1)}, f32[256,1024]{1,0:T(8,128)}, u32[]{:S(2)}) copy-start(f32[256,1024]{1,0:T(8,128)} %copy-done.5) | copy-start | bytes 3145732
  352.8 4.6 %copy-start.3 = (bf16[4,64,1664]{2,1,0:T(8,128)(2,1)}, bf16[4,64,1664]{2,1,0:T(8,128)(2,1)S(1)}, u32[]{:S(2)}) copy-start(bf16[4,64,1664]{2,1,0:T(8,128)(2,1)S(1)} %get-tuple-element.55.packed) | copy-start | bytes 2555908
  352.8 3.4 copy-start.9
  352.8 3.4 copy-start.11
  352.8 3.4 copy-start.25
  355.3 3.6 collective-permute-start.6
  407.1 1.4 copy-start.29
  409.3 7.4 %copy-start.1 = (bf16[32,16,1024]{2,1,0:T(8,128)(2,1)S(1)}, bf16[32,16,1024]{2,1,0:T(8,128)(2,1)}, u32[]{:S(2)}) copy-start(bf16[32,16,1024]{2,1,0:T(8,128)(2,1)} %param.20) | copy-start | bytes 3145732
Sparse Core Ops, SparseCore 0:
  47.9 113.8 all-gather.1
  218.2 108.9 reduce-scatter.1
